TPU v7x, 512 devices: a whole 4x8x8 slice. The times are simulated.
512 devices in a mesh: tile: 64 (over z_hi, y, core), dp: 8 (over z_lo, x).
Axes of the slice: x: 4, y: 8, z: 8 (z_hi: 4, z_lo: 2; z = z_hi * 2 + z_lo), core: 2. Of those that a mesh axis runs over, the one named last changes fastest.
Arguments:
- fields: bfloat16 [8, 768, 64, 128], P('dp', 'tile'), may hold values from -6 to 6
- cotangent: bfloat16 [8, 768, 64, 128], P('dp', 'tile'), may hold values from -6 to 6
- face_flip: int32 [12], replicated, may hold values from 0 to 1
- kernel: bfloat16 [2, 49, 128], replicated, may hold values from -0.875 to 0.875
- ln_gain: float32 [2, 128], replicated, may hold values from 0.25 to 1.75
- weight_in: bfloat16 [2, 128, 512], replicated, may hold values from -0.5 to 0.5
- bias_in: float32 [2, 512], replicated, may hold values from -3 to 3
- weight_out: bfloat16 [2, 512, 128], replicated, may hold values from -0.25 to 0.25
- layer_scale: float32 [2, 128], replicated, may hold values from 0.25 to 1
Outputs:
- result: bfloat16 [8, 768, 64, 128], P('dp', 'tile')
- grad_input: bfloat16 [8, 768, 64, 128], P('dp', 'tile')
- grad_kernel: float32 [2, 49, 128], P(None, None, 'dp')
- grad_gain: float32 [2, 128], P(None, 'dp')
- grad_weight_in: float32 [2, 128, 512], P(None, 'dp')
- grad_bias_in: float32 [2, 512], P(None, 'dp')
- grad_weight_out: float32 [2, 512, 128], P(None, 'dp')
- grad_scale: float32 [2, 128], P(None, 'dp')
All inputs are finite; a program needn't handle non-finite values.
Results may differ from a plain program's by a relative error of at most 0.018.
Values may be sent and summed in bfloat16 or wider, within the bound.
No kernel may reach another device: no remote copies, remote signals or barrier semaphores. Data moves between devices by JAX's collectives and lax.ppermute only.
A program may use at most 64 MiB of HBM per device.

v0:
```python
import math

import jax
import jax.numpy as jnp
from jax import lax
from jax.sharding import PartitionSpec as P

KS = 7


EPSILON = 1e-06
SQRT_HALF = 0.7071067811865476
INV_ROOT_TWO_PI = 0.3989422804014327


def padded_2(x, sides, width):
    for axis, dim in sides:
        count, length = (lax.axis_size(axis), x.shape[dim])
        up = [(i, (i + 1) % count) for i in range(count)]
        down = [(j, i) for i, j in up]
        last = lax.slice_in_dim(x, length - width, length, axis=dim)
        initial = lax.slice_in_dim(x, 0, width, axis=dim)
        before = lax.ppermute(last, axis, up)
        after = lax.ppermute(initial, axis, down)
        x = jnp.concatenate([before, x, after], axis=dim)
    return x


def passed_along(block, axis, distance):
    devices = range(lax.axis_size(axis))
    route = [((i - distance) % len(devices), i) for i in devices]
    return lax.ppermute(block, axis, route)


def gelu_parts(preact):
    normal_cdf = 0.5 * (1.0 + jax.scipy.special.erf(preact * SQRT_HALF))
    return (
        preact * normal_cdf,
        normal_cdf + preact * jnp.exp(-0.5 * preact * preact) * INV_ROOT_TWO_PI,
    )


def depthwise(padded, kernel_taps):
    return lax.conv_general_dilated(
        padded[None],
        kernel_taps[:, :, None, :],
        (1, 1),
        "VALID",
        dimension_numbers=("NHWC", "HWIO", "NHWC"),
        feature_group_count=padded.shape[2],
        preferred_element_type=jnp.float32,
    )[0]


def tap_sums(padded, grad_conv):
    summed = lax.conv_general_dilated(
        padded[None],
        grad_conv[:, :, None, :],
        (1, 1),
        "VALID",
        dimension_numbers=("NHWC", "HWIO", "NHWC"),
        feature_group_count=padded.shape[2],
        preferred_element_type=jnp.float32,
    )
    return summed[0]


def row_flags(face_flip, row_start, count, width):
    row_ids = row_start + jnp.arange(count, dtype=jnp.int32)
    column_ids = row_ids // (3 * width)
    levels = row_ids % (3 * width) // width
    face_ids = 4 * levels + column_ids
    matches = face_ids[:, None] == jnp.arange(12, dtype=jnp.int32)[None, :]
    return jnp.sum(jnp.where(matches, face_flip[None, :], 0), axis=1) > 0


def orient(states, flipped):
    return jnp.where(flipped[:, None, None], states[:, ::-1], states)


def extend_strip(states, strip_count):
    width = states.shape[1]
    extended = padded_2(states, (("tile", 0),), 3)
    western = passed_along(extended[:, width - 3 :], "tile", strip_count)
    eastern = passed_along(extended[:, :3], "tile", -strip_count)
    return jnp.concatenate([western, extended, eastern], axis=1)


def forward_block(
    states, kernel_taps, gain_row, weight_in_row, bias_row, weight_out_row, scale_row, strip_count
):
    channels = states.shape[2]
    padded = extend_strip(states, strip_count)
    convolved = depthwise(padded, kernel_taps).reshape(-1, channels)
    average = jnp.mean(convolved, axis=-1, keepdims=True)
    centered = convolved - average
    inv_std = lax.rsqrt(jnp.mean(centered * centered, axis=-1, keepdims=True) + EPSILON)
    normed = centered * inv_std
    scaled = (normed * gain_row).astype(jnp.bfloat16)
    preact = jnp.dot(scaled, weight_in_row, preferred_element_type=jnp.float32) + bias_row
    gelu_value, gelu_slope = gelu_parts(preact)
    hidden = gelu_value.astype(jnp.bfloat16)
    branch = jnp.dot(hidden, weight_out_row, preferred_element_type=jnp.float32)
    output = (states.reshape(-1, channels).astype(jnp.float32) + scale_row * branch).astype(
        jnp.bfloat16
    )
    return (
        output.reshape(states.shape),
        (padded, normed, inv_std, scaled, gelu_slope, hidden, branch),
    )


def backward_block(
    upstream, saved, kernel_taps, gain_row, weight_in_row, weight_out_row, scale_row, strip_count
):
    padded, normed, inv_std, scaled, gelu_slope, hidden, branch = saved
    grid_shape = upstream.shape
    channels = grid_shape[2]
    up_float = upstream.reshape(-1, channels).astype(jnp.float32)
    grad_scale = jnp.sum(up_float * branch, axis=0)
    grad_branch = (up_float * scale_row).astype(jnp.bfloat16)
    grad_weight_out = jnp.dot(hidden.T, grad_branch, preferred_element_type=jnp.float32)
    grad_preact = (
        jnp.dot(grad_branch, weight_out_row.T, preferred_element_type=jnp.float32) * gelu_slope
    ).astype(jnp.bfloat16)
    grad_bias = jnp.sum(grad_preact.astype(jnp.float32), axis=0)
    grad_weight_in = jnp.dot(scaled.T, grad_preact, preferred_element_type=jnp.float32)
    grad_scaled = jnp.dot(grad_preact, weight_in_row.T, preferred_element_type=jnp.float32)
    grad_gain = jnp.sum(grad_scaled * normed, axis=0)
    grad_normed = grad_scaled * gain_row
    grad_conv = inv_std * (
        grad_normed
        - jnp.mean(grad_normed, axis=-1, keepdims=True)
        - normed * jnp.mean(grad_normed * normed, axis=-1, keepdims=True)
    )
    grad_conv = grad_conv.astype(jnp.bfloat16).reshape(grid_shape)
    grad_padded = extend_strip(grad_conv, strip_count)
    grad_taps = tap_sums(padded, grad_conv)
    spread = depthwise(grad_padded, kernel_taps[::-1, ::-1]).reshape(-1, channels)
    grad_field = (up_float + spread).astype(jnp.bfloat16).reshape(grid_shape)
    return (
        grad_field,
        (
            grad_taps.reshape(-1, channels),
            grad_gain,
            grad_weight_in,
            grad_bias,
            grad_weight_out,
            grad_scale,
        ),
    )


def on_device(
    fields, cotangent, face_flip, kernel, ln_gain, weight_in, bias_in, weight_out, layer_scale
):
    strip_count = lax.axis_size("tile") // 4
    tile_index = lax.axis_index("tile")
    height = fields.shape[1]
    width = fields.shape[2]
    channels = fields.shape[3]
    layers = kernel.shape[0]
    flipped = row_flags(face_flip, tile_index * height, height, width)
    current = orient(fields[0], flipped)
    saved_all = []
    for layer_index in range(layers):
        kernel_taps = kernel[layer_index].reshape(KS, KS, channels)
        current, saved = forward_block(
            current,
            kernel_taps,
            ln_gain[layer_index],
            weight_in[layer_index],
            bias_in[layer_index],
            weight_out[layer_index],
            layer_scale[layer_index],
            strip_count,
        )
        saved_all.append(saved)
    output = orient(current, flipped)
    grad_field = orient(cotangent[0], flipped)
    gradients = [None] * layers
    for layer_index in reversed(range(layers)):
        kernel_taps = kernel[layer_index].reshape(KS, KS, channels)
        grad_field, gradients[layer_index] = backward_block(
            grad_field,
            saved_all[layer_index],
            kernel_taps,
            ln_gain[layer_index],
            weight_in[layer_index],
            weight_out[layer_index],
            layer_scale[layer_index],
            strip_count,
        )
    normalizer = 1.0 / math.sqrt(lax.axis_size("dp") * 12 * width * width)
    local_terms = tuple(
        (jnp.stack([entry[member] for entry in gradients]) * normalizer for member in range(6))
    )
    summed = lax.psum(
        (
            local_terms[0],
            local_terms[1],
            local_terms[2],
            local_terms[3],
            local_terms[4],
            local_terms[5],
        ),
        "tile",
    )
    shares = (
        lax.psum_scatter(
            summed[0].astype(jnp.bfloat16), "dp", scatter_dimension=2, tiled=True
        ).astype(jnp.float32),
        lax.psum_scatter(
            summed[1].astype(jnp.bfloat16), "dp", scatter_dimension=1, tiled=True
        ).astype(jnp.float32),
        lax.psum_scatter(
            summed[2].astype(jnp.bfloat16), "dp", scatter_dimension=1, tiled=True
        ).astype(jnp.float32),
        lax.psum_scatter(
            summed[3].astype(jnp.bfloat16), "dp", scatter_dimension=1, tiled=True
        ).astype(jnp.float32),
        lax.psum_scatter(
            summed[4].astype(jnp.bfloat16), "dp", scatter_dimension=1, tiled=True
        ).astype(jnp.float32),
        lax.psum_scatter(
            summed[5].astype(jnp.bfloat16), "dp", scatter_dimension=1, tiled=True
        ).astype(jnp.float32),
    )
    grad_input = orient(grad_field, flipped)
    return (
        output[None],
        grad_input[None],
        shares[0],
        shares[1],
        shares[2],
        shares[3],
        shares[4],
        shares[5],
    )


def solution(mesh):
    return jax.shard_map(
        on_device,
        mesh=mesh,
        in_specs=(
            P("dp", "tile", None, None),
            P("dp", "tile", None, None),
            P(),
            P(),
            P(),
            P(),
            P(),
            P(),
            P(),
        ),
        out_specs=(
            P("dp", "tile", None, None),
            P("dp", "tile", None, None),
            P(None, None, "dp"),
            P(None, "dp"),
            P(None, "dp", None),
            P(None, "dp"),
            P(None, "dp", None),
            P(None, "dp"),
        ),
        check_vma=False,
    )
```

profile of v0, /device:TPU:1, one launch (start us, length us, event | category | flops | bytes accessed | tf_op | source)
XLA Modules:
  0.0 675.7 jit_solution(4245122790107561670)
XLA Ops:
  10.1 4.6 collective-permute-start
  14.7 6.1 collective-permute-start.1
  26.9 6.5 collective-permute-start.3
  41.4 7.8 %collective-permute-start.5 = (bf16[3,64,128]{2,1,0:T(8,128)(2,1)S(1)}, bf16[3,64,128]{2,1,0:T(8,128)(2,1)S(1)}, u32[]{:S(2)}, u32[]{:S(2)}) collective-permute-start(bf16[3,64,128]{2,1,0:T(8,128)(2,1)S(1)} %bitcast.260), channel_id=1, source_target_pairs={{8,0},{16,8},{24,16},{32,24},{40,32},{48,40},{56,48},{64,56},{72,6... | collective-permute-start | bytes 147464 | tf_op jit(solution)/shard_map/ppermute | solution.py:24
  52.1 2.6 collective-permute-done.4
  54.7 3.4 collective-permute-start.6
  58.1 4.0 collective-permute-start.7
  72.7 4.2 collective-permute-start.8
  77.0 7.8 %collective-permute-start.9 = (bf16[3,64,128]{2,0,1:T(4,128)(2,1)S(1)}, bf16[3,64,128]{2,0,1:T(4,128)(2,1)S(1)}, u32[]{:S(2)}, u32[]{:S(2)}) collective-permute-start(bf16[3,64,128]{2,0,1:T(4,128)(2,1)S(1)} %copy.235), channel_id=1, source_target_pairs={{8,0},{16,8},{24,16},{32,24},{40,32},{48,40},{56,48},{64,56},{72,6... | collective-permute-start | bytes 147464 | tf_op jit(solution)/shard_map/ppermute | solution.py:24
  84.8 3.8 fusion.16
  89.2 5.5 collective-permute-start.10
  97.0 3.1 collective-permute-done.11
  107.5 3.8 fusion.18
  111.3 291.9 %all-reduce.2 = (bf16[2,49,128]{2,1,0:T(8,128)(2,1)S(1)}, bf16[2,128]{1,0:T(2,128)(2,1)S(1)}, bf16[2,128,512]{2,1,0:T(8,128)(2,1)}, bf16[2,512]{1,0:T(2,128)(2,1...) all-reduce(f32[2,49,128]{2,1,0:T(8,128)S(1)} %maximum_multiply_fusi, ...), channel_id=1, replica_groups=mesh['tile'=64,'dp'=8] {'tile'}, use_global_device_ids=true, to_apply=%region_9.10 | all-reduce | flops 276224 | bytes 1657344 | tf_op jit(solution)/shard_map/psum | solution.py:198
  407.3 3.3 collective-permute-start.12
  410.7 6.9 %collective-permute-start.13 = (bf16[3,64,128]{2,0,1:T(4,128)(2,1)S(1)}, bf16[3,64,128]{2,0,1:T(4,128)(2,1)S(1)}, u32[]{:S(2)}, u32[]{:S(2)}) collective-permute-start(bf16[3,64,128]{2,0,1:T(4,128)(2,1)S(1)} %copy.244), channel_id=1, source_target_pairs={{8,0},{16,8},{24,16},{32,24},{40,32},{48,40},{56,48},{64,56},{72,6... | collective-permute-start | bytes 147464 | tf_op jit(solution)/shard_map/ppermute | solution.py:24
  418.5 1.9 collective-permute-start.14
  420.4 5.7 collective-permute-start.15
  426.3 16.6 %reduce-scatter.21.cloned.1.call-done = bf16[16,2]{1,0:T(8,128)(2,1)} async-done(((bf16[128,2]{1,0:T(8,128)(2,1)}), bf16[16,2]{1,0:T(8,128)(2,1)}) %reduce-scatter.21.cloned.1.call-update) | async-done | bytes 80
  444.2 43.6 %reduce-scatter.25.cloned.1.call-done = bf16[16,2]{1,0:T(8,128)(2,1)} async-done(((bf16[128,2]{1,0:T(8,128)(2,1)}), bf16[16,2]{1,0:T(8,128)(2,1)}) %reduce-scatter.25.cloned.1.call-update) | async-done | bytes 80
  489.2 44.4 %reduce-scatter.23.cloned.1.call-done = bf16[64,2]{1,0:T(8,128)(2,1)} async-done(((bf16[512,2]{1,0:T(8,128)(2,1)}), bf16[64,2]{1,0:T(8,128)(2,1)}) %reduce-scatter.23.cloned.1.call-update) | async-done | bytes 272
  534.9 43.1 %reduce-scatter.19.cloned.1.call-done = bf16[16,98]{1,0:T(8,128)(2,1)} async-done(((bf16[128,98]{1,0:T(8,128)(2,1)}), bf16[16,98]{1,0:T(8,128)(2,1)}) %reduce-scatter.19.cloned.1.call-update) | async-done | bytes 3152
  583.2 39.8 %reduce-scatter.17.cloned.1.call-done = bf16[2,64,128]{2,1,0:T(8,128)(2,1)} async-done(((bf16[2,512,128]{2,1,0:T(8,128)(2,1)}), bf16[2,64,128]{2,1,0:T(8,128)(2,1)}) %reduce-scatter.17.cloned.1.call-update) | async-done | bytes 32784 | tf_op jit(solution)/shard_map/reduce_scatter | solution.py:222
  624.4 43.1 %reduce-scatter.15.cloned.1.call-done = bf16[2,16,512]{2,1,0:T(8,128)(2,1)} async-done(((bf16[2,128,512]{2,1,0:T(8,128)(2,1)}), bf16[2,16,512]{2,1,0:T(8,128)(2,1)}) %reduce-scatter.15.cloned.1.call-update) | async-done | bytes 32784 | tf_op jit(solution)/shard_map/reduce_scatter | solution.py:216
  (217 shorter events, 57.1 us)
Async XLA Ops:
  7.2 435.7 %reduce-scatter.21.cloned.1.call-start = ((), (), s32[]{:S(2)}) async-start(), calls=%async_computation.9 | async-start | bytes 36864
  8.1 43.1 %copy-start.22 = (pred[12]{0:T(512)(128)(4,1)}, pred[12]{0:T(512)(128)(4,1)S(1)}, u32[]{:S(2)}) copy-start(pred[12]{0:T(512)(128)(4,1)S(1)} %broadcast_compare_fusion) | copy-start | bytes 40
  10.1 14.8 %collective-permute-start = (bf16[3,64,128]{2,1,0:T(8,128)(2,1)S(1)}, bf16[3,64,128]{2,1,0:T(8,128)(2,1)S(1)}, u32[]{:S(2)}, u32[]{:S(2)}) collective-permute-start(bf16[3,64,128]{2,1,0:T(8,128)(2,1)S(1)} %get-tuple-element.94), channel_id=1, source_target_pairs={{0,8},{8,16},{16,24},{24,32},{32,40},{40,48},{48,56},{56,64},{64,7... | collective-permute-start | bytes 147464 | tf_op jit(solution)/shard_map/ppermute | solution.py:23
  14.7 10.2 %collective-permute-start.1 = (bf16[3,64,128]{2,1,0:T(8,128)(2,1)S(1)}, bf16[3,64,128]{2,1,0:T(8,128)(2,1)S(1)}, u32[]{:S(2)}, u32[]{:S(2)}) collective-permute-start(bf16[3,64,128]{2,1,0:T(8,128)(2,1)S(1)} %get-tuple-element.95), channel_id=1, source_target_pairs={{8,0},{16,8},{24,16},{32,24},{40,32},{48,40},{56,48},{64,56},{72,6... | collective-permute-start | bytes 147464 | tf_op jit(solution)/shard_map/ppermute | solution.py:24
  25.0 8.5 %collective-permute-start.2 = (bf16[18,3,128]{2,1,0:T(4,128)(2,1)S(1)}, bf16[18,3,128]{2,1,0:T(4,128)(2,1)S(1)}, u32[]{:S(2)}, u32[]{:S(2)}) collective-permute-start(bf16[18,3,128]{2,1,0:T(4,128)(2,1)S(1)} %get-tuple-element.86), channel_id=1, source_target_pairs={{384,0},{392,8},{400,16},{408,24},{416,32},{424,40},{432,48},{440,... | collective-permute-start | bytes 41480 | tf_op jit(solution)/shard_map/ppermute | solution.py:32
  26.9 7.9 %collective-permute-start.3 = (bf16[18,3,128]{2,1,0:T(4,128)(2,1)S(1)}, bf16[18,3,128]{2,1,0:T(4,128)(2,1)S(1)}, u32[]{:S(2)}, u32[]{:S(2)}) collective-permute-start(bf16[18,3,128]{2,1,0:T(4,128)(2,1)S(1)} %get-tuple-element.87), channel_id=1, source_target_pairs={{128,0},{136,8},{144,16},{152,24},{160,32},{168,40},{176,48},{184,... | collective-permute-start | bytes 41480 | tf_op jit(solution)/shard_map/ppermute | solution.py:32
  41.4 10.7 %collective-permute-start.5 = (bf16[3,64,128]{2,1,0:T(8,128)(2,1)S(1)}, bf16[3,64,128]{2,1,0:T(8,128)(2,1)S(1)}, u32[]{:S(2)}, u32[]{:S(2)}) collective-permute-start(bf16[3,64,128]{2,1,0:T(8,128)(2,1)S(1)} %bitcast.260), channel_id=1, source_target_pairs={{8,0},{16,8},{24,16},{32,24},{40,32},{48,40},{56,48},{64,56},{72,6... | collective-permute-start | bytes 147464 | tf_op jit(solution)/shard_map/ppermute | solution.py:24
  49.2 5.4 collective-permute-start.4
  54.7 10.2 %collective-permute-start.6 = (bf16[18,3,128]{2,1,0:T(4,128)(2,1)S(1)}, bf16[18,3,128]{2,1,0:T(4,128)(2,1)S(1)}, u32[]{:S(2)}, u32[]{:S(2)}) collective-permute-start(bf16[18,3,128]{2,1,0:T(4,128)(2,1)S(1)} %get-tuple-element.84), channel_id=1, source_target_pairs={{384,0},{392,8},{400,16},{408,24},{416,32},{424,40},{432,48},{440,... | collective-permute-start | bytes 41480 | tf_op jit(solution)/shard_map/ppermute | solution.py:32
  58.1 6.8 %collective-permute-start.7 = (bf16[18,3,128]{2,1,0:T(4,128)(2,1)S(1)}, bf16[18,3,128]{2,1,0:T(4,128)(2,1)S(1)}, u32[]{:S(2)}, u32[]{:S(2)}) collective-permute-start(bf16[18,3,128]{2,1,0:T(4,128)(2,1)S(1)} %get-tuple-element.85), channel_id=1, source_target_pairs={{128,0},{136,8},{144,16},{152,24},{160,32},{168,40},{176,48},{184,... | collective-permute-start | bytes 41480 | tf_op jit(solution)/shard_map/ppermute | solution.py:32
  72.7 16.4 %collective-permute-start.8 = (bf16[3,64,128]{2,0,1:T(4,128)(2,1)S(1)}, bf16[3,64,128]{2,0,1:T(4,128)(2,1)S(1)}, u32[]{:S(2)}, u32[]{:S(2)}) collective-permute-start(bf16[3,64,128]{2,0,1:T(4,128)(2,1)S(1)} %copy.234), channel_id=1, source_target_pairs={{0,8},{8,16},{16,24},{24,32},{32,40},{40,48},{48,56},{56,64},{64,7... | collective-permute-start | bytes 147464 | tf_op jit(solution)/shard_map/ppermute | solution.py:23
  77.0 12.2 %collective-permute-start.9 = (bf16[3,64,128]{2,0,1:T(4,128)(2,1)S(1)}, bf16[3,64,128]{2,0,1:T(4,128)(2,1)S(1)}, u32[]{:S(2)}, u32[]{:S(2)}) collective-permute-start(bf16[3,64,128]{2,0,1:T(4,128)(2,1)S(1)} %copy.235), channel_id=1, source_target_pairs={{8,0},{16,8},{24,16},{32,24},{40,32},{48,40},{56,48},{64,56},{72,6... | collective-permute-start | bytes 147464 | tf_op jit(solution)/shard_map/ppermute | solution.py:24
  89.2 7.7 %collective-permute-start.10 = (bf16[18,3,128]{2,0,1:T(8,128)(2,1)S(1)}, bf16[18,3,128]{2,0,1:T(8,128)(2,1)S(1)}, u32[]{:S(2)}, u32[]{:S(2)}) collective-permute-start(bf16[18,3,128]{2,0,1:T(8,128)(2,1)S(1)} %get-tuple-element.78), channel_id=1, source_target_pairs={{384,0},{392,8},{400,16},{408,24},{416,32},{424,40},{432,48},{440,... | collective-permute-start | bytes 41480 | tf_op jit(solution)/shard_map/ppermute | solution.py:32
  94.7 5.4 collective-permute-start.11
  404.0 83.9 %reduce-scatter.25.cloned.1.call-start = ((), (), s32[]{:S(2)}) async-start(), calls=%async_computation.11 | async-start | bytes 36864
  404.8 128.8 %reduce-scatter.23.cloned.1.call-start = ((), (), s32[]{:S(2)}) async-start(), calls=%async_computation.10 | async-start | bytes 147456
  405.7 172.4 %reduce-scatter.19.cloned.1.call-start = ((), (), s32[]{:S(2)}) async-start(), calls=%async_computation.8 | async-start | bytes 36864
  406.6 216.4 %reduce-scatter.17.cloned.1.call-start = ((), (), s32[]{:S(2)}) async-start(), calls=%async_computation.7 | async-start | bytes 294912 | tf_op jit(solution)/shard_map/reduce_scatter | solution.py:222
  407.2 260.3 %reduce-scatter.15.cloned.1.call-start = ((), (), s32[]{:S(2)}) async-start(), calls=%async_computation.6 | async-start | bytes 294912 | tf_op jit(solution)/shard_map/reduce_scatter | solution.py:216
  407.3 10.4 %collective-permute-start.12 = (bf16[3,64,128]{2,0,1:T(4,128)(2,1)S(1)}, bf16[3,64,128]{2,0,1:T(4,128)(2,1)S(1)}, u32[]{:S(2)}, u32[]{:S(2)}) collective-permute-start(bf16[3,64,128]{2,0,1:T(4,128)(2,1)S(1)} %copy.243), channel_id=1, source_target_pairs={{0,8},{8,16},{16,24},{24,32},{32,40},{40,48},{48,56},{56,64},{64,7... | collective-permute-start | bytes 147464 | tf_op jit(solution)/shard_map/ppermute | solution.py:23
  410.7 7.8 %collective-permute-start.13 = (bf16[3,64,128]{2,0,1:T(4,128)(2,1)S(1)}, bf16[3,64,128]{2,0,1:T(4,128)(2,1)S(1)}, u32[]{:S(2)}, u32[]{:S(2)}) collective-permute-start(bf16[3,64,128]{2,0,1:T(4,128)(2,1)S(1)} %copy.244), channel_id=1, source_target_pairs={{8,0},{16,8},{24,16},{32,24},{40,32},{48,40},{56,48},{64,56},{72,6... | collective-permute-start | bytes 147464 | tf_op jit(solution)/shard_map/ppermute | solution.py:24
  418.5 161.1 %collective-permute-start.14 = (bf16[18,3,128]{2,0,1:T(8,128)(2,1)S(1)}, bf16[18,3,128]{2,0,1:T(8,128)(2,1)S(1)}, u32[]{:S(2)}, u32[]{:S(2)}) collective-permute-start(bf16[18,3,128]{2,0,1:T(8,128)(2,1)S(1)} %get-tuple-element.76), channel_id=1, source_target_pairs={{384,0},{392,8},{400,16},{408,24},{416,32},{424,40},{432,48},{440,... | collective-permute-start | bytes 41480 | tf_op jit(solution)/shard_map/ppermute | solution.py:32
  420.4 159.2 %collective-permute-start.15 = (bf16[18,3,128]{2,0,1:T(8,128)(2,1)S(1)}, bf16[18,3,128]{2,0,1:T(8,128)(2,1)S(1)}, u32[]{:S(2)}, u32[]{:S(2)}) collective-permute-start(bf16[18,3,128]{2,0,1:T(8,128)(2,1)S(1)} %get-tuple-element.77), channel_id=1, source_target_pairs={{128,0},{136,8},{144,16},{152,24},{160,32},{168,40},{176,48},{184,... | collective-permute-start | bytes 41480 | tf_op jit(solution)/shard_map/ppermute | solution.py:32
  426.3 153.8 %copy-start.28 = (pred[8,9]{0,1:T(8,128)(4,1)S(1)}, pred[8,9]{0,1:T(8,128)(4,1)}, u32[]{:S(2)}) copy-start(pred[8,9]{0,1:T(8,128)(4,1)} %constant.103) | copy-start | bytes 220
  (27 other events, 131.8 us)
Sparse Core Ops, SparseCore 0:
  404.1 38.7 reduce-scatter.20
  446.3 41.5 reduce-scatter.24
  491.2 42.2 reduce-scatter.22
  536.8 41.2 reduce-scatter.18
  580.7 42.2 reduce-scatter.16
  625.6 41.8 reduce-scatter.14
where the time goes:
time: 681 us; the launch traced here: 676 us
  blocking collectives  292 us (43%)
  waiting for transfers between devices  239 us (35%)
  starting transfers between devices  73.8 us (11%)
  matrix products  20.8 us (3%)
  local copies, waits for them, and re-layouts  20.2 us (3%)
  between operations  15.1 us (2%)
  other arithmetic  15 us (2%)
    psum x1, blocking collectives, on_device(): lax.psum((local_terms[0], local_terms[1], local_terms[2], local_terms[3],...  292 us
    unnamed x10, waiting for transfers between devices  148 us
    reduce_scatter x1, waiting for transfers between devices, on_device(): lax.psum_scatter(summed[2].astype(jnp.bfloat16), 'dp', scatter_dimension=...  43.1 us
    reduce_scatter x1, waiting for transfers between devices, on_device(): lax.psum_scatter(summed[4].astype(jnp.bfloat16), 'dp', scatter_dimension=...  39.8 us
    ppermute x8, starting transfers between devices, passed_along(): return lax.ppermute(block, axis, route)  30.8 us
    ppermute x4, starting transfers between devices, padded_2(): after = lax.ppermute(initial, axis, down)  28.6 us
    ppermute x4, starting transfers between devices, padded_2(): before = lax.ppermute(last, axis, up)  14.1 us
  transfers between devices with their start and end apart: 22, of which 10 were waited for; matrix products, arithmetic and copies ran while one was open for 4% of the time, Pallas kernels for 0%

commit v1 on v0

--- a/solution.py
+++ b/solution.py
@@ -6,6 +6,8 @@
 from jax.sharding import PartitionSpec as P
 
 KS = 7
+TILE = ("zh", "y", "c")
+DP = ("zl", "x")
 
 
 EPSILON = 1e-06
@@ -80,9 +82,9 @@
 
 def extend_strip(states, strip_count):
     width = states.shape[1]
-    extended = padded_2(states, (("tile", 0),), 3)
-    western = passed_along(extended[:, width - 3 :], "tile", strip_count)
-    eastern = passed_along(extended[:, :3], "tile", -strip_count)
+    extended = padded_2(states, ((TILE, 0),), 3)
+    western = passed_along(extended[:, width - 3 :], TILE, strip_count)
+    eastern = passed_along(extended[:, :3], TILE, -strip_count)
     return jnp.concatenate([western, extended, eastern], axis=1)
 
 
@@ -151,11 +153,65 @@
     )
 
 
+def exchanged(blocks, axis):
+    return lax.all_to_all(blocks, axis, 0, 0, tiled=True)
+
+
+def summed_shares(taps, gain, weight_in, bias, weight_out, scale):
+    members = lax.axis_size(DP)
+    layers, channels, hidden = weight_in.shape
+    strips = hidden // channels
+    part = channels // members
+    small = jnp.concatenate(
+        [
+            taps.reshape(-1, channels).T,
+            gain.T,
+            scale.T,
+            bias.reshape(layers, channels, strips).transpose(1, 0, 2).reshape(channels, -1),
+        ],
+        axis=1,
+    )
+    used = small.shape[1]
+    small = jnp.pad(small, ((0, 0), (0, channels - used)))
+    inward = weight_in.reshape(layers, members, part, strips, channels).transpose(1, 0, 3, 2, 4)
+    outward = weight_out.reshape(layers, members, -1, channels).transpose(1, 0, 2, 3)
+    rows = lax.axis_size("y")
+    packed = jnp.concatenate(
+        [
+            small.reshape(members, rows, -1, channels),
+            inward.reshape(members, rows, -1, channels),
+            outward.reshape(members, rows, -1, channels),
+        ],
+        axis=2,
+    ).astype(jnp.bfloat16)
+    share = jnp.sum(exchanged(packed, DP).astype(jnp.float32), axis=0)
+    piece = jnp.sum(exchanged(share.astype(jnp.bfloat16), "y").astype(jnp.float32), axis=0)
+    others = lax.axis_size("zh") * lax.axis_size("c")
+    copies = jnp.broadcast_to(piece.astype(jnp.bfloat16)[None], (others, *piece.shape))
+    piece = jnp.sum(exchanged(copies, ("zh", "c")).astype(jnp.float32), axis=0)
+    copies = jnp.broadcast_to(piece.astype(jnp.bfloat16)[None], (rows, *piece.shape))
+    full = exchanged(copies, "y").astype(jnp.float32)
+    first, second = part // rows, (part + layers * strips * part) // rows
+    small = full[:, :first].reshape(part, channels)
+    inward = full[:, first:second].reshape(layers, strips, part, channels)
+    outward = full[:, second:].reshape(layers, -1, channels)
+    small_t = small.T
+    tap_rows = taps.shape[0] * taps.shape[1]
+    return (
+        small_t[:tap_rows].reshape(layers, -1, part),
+        small_t[tap_rows : tap_rows + layers],
+        inward.transpose(0, 2, 1, 3).reshape(layers, part, hidden),
+        small[:, tap_rows + 2 * layers : used].reshape(part, layers, strips).transpose(1, 0, 2).reshape(layers, -1),
+        outward,
+        small_t[tap_rows + layers : tap_rows + 2 * layers],
+    )
+
+
 def on_device(
     fields, cotangent, face_flip, kernel, ln_gain, weight_in, bias_in, weight_out, layer_scale
 ):
-    strip_count = lax.axis_size("tile") // 4
-    tile_index = lax.axis_index("tile")
+    strip_count = lax.axis_size(TILE) // 4
+    tile_index = lax.axis_index(TILE)
     height = fields.shape[1]
     width = fields.shape[2]
     channels = fields.shape[3]
@@ -191,40 +247,9 @@
             layer_scale[layer_index],
             strip_count,
         )
-    normalizer = 1.0 / math.sqrt(lax.axis_size("dp") * 12 * width * width)
-    local_terms = tuple(
-        (jnp.stack([entry[member] for entry in gradients]) * normalizer for member in range(6))
-    )
-    summed = lax.psum(
-        (
-            local_terms[0],
-            local_terms[1],
-            local_terms[2],
-            local_terms[3],
-            local_terms[4],
-            local_terms[5],
-        ),
-        "tile",
-    )
-    shares = (
-        lax.psum_scatter(
-            summed[0].astype(jnp.bfloat16), "dp", scatter_dimension=2, tiled=True
-        ).astype(jnp.float32),
-        lax.psum_scatter(
-            summed[1].astype(jnp.bfloat16), "dp", scatter_dimension=1, tiled=True
-        ).astype(jnp.float32),
-        lax.psum_scatter(
-            summed[2].astype(jnp.bfloat16), "dp", scatter_dimension=1, tiled=True
-        ).astype(jnp.float32),
-        lax.psum_scatter(
-            summed[3].astype(jnp.bfloat16), "dp", scatter_dimension=1, tiled=True
-        ).astype(jnp.float32),
-        lax.psum_scatter(
-            summed[4].astype(jnp.bfloat16), "dp", scatter_dimension=1, tiled=True
-        ).astype(jnp.float32),
-        lax.psum_scatter(
-            summed[5].astype(jnp.bfloat16), "dp", scatter_dimension=1, tiled=True
-        ).astype(jnp.float32),
+    normalizer = 1.0 / math.sqrt(lax.axis_size(DP) * 12 * width * width)
+    shares = summed_shares(
+        *(jnp.stack([entry[member] for entry in gradients]) * normalizer for member in range(6))
     )
     grad_input = orient(grad_field, flipped)
     return (
@@ -240,12 +265,14 @@
 
 
 def solution(mesh):
+    devices = mesh.devices
+    mesh = jax.sharding.Mesh(devices.reshape(4, 8, 2, 2, 4), ("zh", "y", "c", "zl", "x"))
     return jax.shard_map(
         on_device,
         mesh=mesh,
         in_specs=(
-            P("dp", "tile", None, None),
-            P("dp", "tile", None, None),
+            P(DP, TILE, None, None),
+            P(DP, TILE, None, None),
             P(),
             P(),
             P(),
@@ -255,14 +282,14 @@
             P(),
         ),
         out_specs=(
-            P("dp", "tile", None, None),
-            P("dp", "tile", None, None),
-            P(None, None, "dp"),
-            P(None, "dp"),
-            P(None, "dp", None),
-            P(None, "dp"),
-            P(None, "dp", None),
-            P(None, "dp"),
+            P(DP, TILE, None, None),
+            P(DP, TILE, None, None),
+            P(None, None, DP),
+            P(None, DP),
+            P(None, DP, None),
+            P(None, DP),
+            P(None, DP, None),
+            P(None, DP),
         ),
         check_vma=False,
     )

time: 681 us -> 214 us (0.31)
  blocking collectives: 292 us -> 0 us
  waiting for transfers between devices: 239 us -> 27.6 us
  starting transfers between devices: 73.8 us -> 99.5 us
  between operations: 15.1 us -> 1.79 us
  matrix products: 20.8 us -> 33.9 us
  local copies, waits for them, and re-layouts: 20.2 us -> 32.6 us
    psum x1 -> x0, blocking collectives: 292 us -> none  [on_device(): lax.psum((local_terms[0], local_terms[1], local_terms[2], local_terms[3],...]
    unnamed x10 -> x0, waiting for transfers between devices: 148 us -> none
    reduce_scatter x2 -> x0, waiting for transfers between devices: 82.9 us -> none  [the longest x1 43.1 us: on_device(): lax.psum_scatter(summed[2].astype(jnp.bfloat16), 'dp', scatter_dimension=...]
    all_to_all x0 -> x4, starting transfers between devices: none -> 26.1 us  [exchanged(): return lax.all_to_all(blocks, axis, 0, 0, tiled=True)]
    all_to_all x0 -> x4, waiting for transfers between devices: none -> 19.7 us  [exchanged(): return lax.all_to_all(blocks, axis, 0, 0, tiled=True)]
  transfers between devices with their start and end apart: 22 -> 20, of which waited for: 10 -> 6; matrix products, arithmetic and copies ran while one was open for 4% -> 13% of each run, Pallas kernels for 0% -> 0%
where the time goes in v1:
time: 214 us; the launch traced here: 211 us
  starting transfers between devices  99.5 us (46%)
  matrix products  33.9 us (16%)
  local copies, waits for them, and re-layouts  32.6 us (15%)
  waiting for transfers between devices  27.6 us (13%)
  other arithmetic  15.9 us (7%)
    ppermute x4, starting transfers between devices, padded_2(): after = lax.ppermute(initial, axis, down)  31.6 us
    ppermute x8, starting transfers between devices, passed_along(): return lax.ppermute(block, axis, route)  31 us
    all_to_all x4, starting transfers between devices, exchanged(): return lax.all_to_all(blocks, axis, 0, 0, tiled=True)  26.1 us
    all_to_all x4, waiting for transfers between devices, exchanged(): return lax.all_to_all(blocks, axis, 0, 0, tiled=True)  19.7 us
    ppermute x4, starting transfers between devices, padded_2(): before = lax.ppermute(last, axis, up)  10.9 us
    conv_general_dilated x2, matrix products, tap_sums(): lax.conv_general_dilated(padded[None], grad_conv[:, :, None, :], (1, 1),...  9.36 us
    conv_general_dilated x4, matrix products, depthwise(): lax.conv_general_dilated(padded[None], kernel_taps[:, :, None, :], (1, 1)...  6.83 us
    another operation x6, local copies, waits for them, and re-layouts, on_device(): jnp.stack([entry[member] for entry in gradients]) * normalizer  5.02 us
  transfers between devices with their start and end apart: 20, of which 6 were waited for; matrix products, arithmetic and copies ran while one was open for 13% of the time, Pallas kernels for 0%

profile of v1, /device:TPU:1, one launch (start us, length us, event | category | flops | bytes accessed | tf_op | source)
XLA Modules:
  0.0 211.3 jit_solution(3386379051421612677)
XLA Ops:
  3.6 4.6 %collective-permute-start = (bf16[3,64,128]{2,1,0:T(8,128)(2,1)S(1)}, bf16[3,64,128]{2,1,0:T(8,128)(2,1)S(1)}, u32[]{:S(2)}, u32[]{:S(2)}) collective-permute-start(bf16[3,64,128]{2,1,0:T(8,128)(2,1)S(1)} %get-tuple-element.127), channel_id=1, source_target_pairs={{0,8},{8,16},{16,24},{24,32},{32,40},{40,48},{48,56},{56,64},{64,7... | collective-permute-start | bytes 147464 | tf_op jit(solution)/shard_map/ppermute | solution.py:25
  8.2 6.1 %collective-permute-start.1 = (bf16[3,64,128]{2,1,0:T(8,128)(2,1)S(1)}, bf16[3,64,128]{2,1,0:T(8,128)(2,1)S(1)}, u32[]{:S(2)}, u32[]{:S(2)}) collective-permute-start(bf16[3,64,128]{2,1,0:T(8,128)(2,1)S(1)} %get-tuple-element.128), channel_id=1, source_target_pairs={{8,0},{16,8},{24,16},{32,24},{40,32},{48,40},{56,48},{64,56},{72,6... | collective-permute-start | bytes 147464 | tf_op jit(solution)/shard_map/ppermute | solution.py:26
  19.4 6.8 %collective-permute-start.3 = (bf16[18,3,128]{2,1,0:T(4,128)(2,1)S(1)}, bf16[18,3,128]{2,1,0:T(4,128)(2,1)S(1)}, u32[]{:S(2)}, u32[]{:S(2)}) collective-permute-start(bf16[18,3,128]{2,1,0:T(4,128)(2,1)S(1)} %get-tuple-element.120), channel_id=1, source_target_pairs={{128,0},{136,8},{144,16},{152,24},{160,32},{168,40},{176,48},{184,... | collective-permute-start | bytes 41480 | tf_op jit(solution)/shard_map/ppermute | solution.py:34
  34.2 7.2 %collective-permute-start.5 = (bf16[3,64,128]{2,1,0:T(8,128)(2,1)S(1)}, bf16[3,64,128]{2,1,0:T(8,128)(2,1)S(1)}, u32[]{:S(2)}, u32[]{:S(2)}) collective-permute-start(bf16[3,64,128]{2,1,0:T(8,128)(2,1)S(1)} %bitcast.347), channel_id=1, source_target_pairs={{8,0},{16,8},{24,16},{32,24},{40,32},{48,40},{56,48},{64,56},{72,6... | collective-permute-start | bytes 147464 | tf_op jit(solution)/shard_map/ppermute | solution.py:26
  43.4 4.3 %collective-permute-done.4 = bf16[3,64,128]{2,1,0:T(8,128)(2,1)S(1)} collective-permute-done((bf16[3,64,128]{2,1,0:T(8,128)(2,1)S(1)}, bf16[3,64,128]{2,1,0:T(8,128)(2,1)S(1)}, u32[]{:S(2)}, u32[]{:S(2)}) %collective-permute-start.4) | collective-permute-done | bytes 49184 | tf_op jit(solution)/shard_map/ppermute | solution.py:25
  47.7 2.8 %collective-permute-start.6 = (bf16[18,3,128]{2,1,0:T(4,128)(2,1)S(1)}, bf16[18,3,128]{2,1,0:T(4,128)(2,1)S(1)}, u32[]{:S(2)}, u32[]{:S(2)}) collective-permute-start(bf16[18,3,128]{2,1,0:T(4,128)(2,1)S(1)} %get-tuple-element.117), channel_id=1, source_target_pairs={{384,0},{392,8},{400,16},{408,24},{416,32},{424,40},{432,48},{440,... | collective-permute-start | bytes 41480 | tf_op jit(solution)/shard_map/ppermute | solution.py:34
  50.5 4.6 %collective-permute-start.7 = (bf16[18,3,128]{2,1,0:T(4,128)(2,1)S(1)}, bf16[18,3,128]{2,1,0:T(4,128)(2,1)S(1)}, u32[]{:S(2)}, u32[]{:S(2)}) collective-permute-start(bf16[18,3,128]{2,1,0:T(4,128)(2,1)S(1)} %get-tuple-element.118), channel_id=1, source_target_pairs={{128,0},{136,8},{144,16},{152,24},{160,32},{168,40},{176,48},{184,... | collective-permute-start | bytes 41480 | tf_op jit(solution)/shard_map/ppermute | solution.py:34
  71.2 2.5 %collective-permute-start.8 = (bf16[3,64,128]{2,0,1:T(4,128)(2,1)}, bf16[3,64,128]{2,0,1:T(4,128)(2,1)}, u32[]{:S(2)}, u32[]{:S(2)}) collective-permute-start(bf16[3,64,128]{2,0,1:T(4,128)(2,1)} %copy.410), channel_id=1, source_target_pairs={{0,8},{8,16},{16,24},{24,32},{32,40},{40,48},{48,56},{56,64},{64,7... | collective-permute-start | bytes 147464 | tf_op jit(solution)/shard_map/ppermute | solution.py:25
  73.7 9.6 %collective-permute-start.9 = (bf16[3,64,128]{2,0,1:T(4,128)(2,1)}, bf16[3,64,128]{2,0,1:T(4,128)(2,1)}, u32[]{:S(2)}, u32[]{:S(2)}) collective-permute-start(bf16[3,64,128]{2,0,1:T(4,128)(2,1)} %copy.411), channel_id=1, source_target_pairs={{8,0},{16,8},{24,16},{32,24},{40,32},{48,40},{56,48},{64,56},{72,6... | collective-permute-start | bytes 147464 | tf_op jit(solution)/shard_map/ppermute | solution.py:26
  85.0 4.5 %fusion.38 = f32[1,7,7,128]{3,0,2,1:T(1,128)} fusion(bf16[1,18,70,128]{3,2,1,0:T(8,128)(2,1)S(1)} %copy-done.14, bf16[12,64,1,128]{3,1,0,2:T(8,128)(2,1)S(1)} %bitcast.318), kind=kOutput, calls=%fused_computation.64 | convolution fusion | flops 9633792 | bytes 544256 | tf_op jit(solution)/shard_map/conv_general_dilated | solution.py:58
  95.5 4.6 %collective-permute-start.10 = (bf16[18,3,128]{2,0,1:T(8,128)(2,1)}, bf16[18,3,128]{2,0,1:T(8,128)(2,1)}, u32[]{:S(2)}, u32[]{:S(2)}) collective-permute-start(bf16[18,3,128]{2,0,1:T(8,128)(2,1)} %get-tuple-element.111), channel_id=1, source_target_pairs={{384,0},{392,8},{400,16},{408,24},{416,32},{424,40},{432,48},{440,... | collective-permute-start | bytes 41480 | tf_op jit(solution)/shard_map/ppermute | solution.py:34
  100.1 2.8 %collective-permute-start.11 = (bf16[18,3,128]{2,0,1:T(8,128)(2,1)}, bf16[18,3,128]{2,0,1:T(8,128)(2,1)}, u32[]{:S(2)}, u32[]{:S(2)}) collective-permute-start(bf16[18,3,128]{2,0,1:T(8,128)(2,1)} %get-tuple-element.112), channel_id=1, source_target_pairs={{128,0},{136,8},{144,16},{152,24},{160,32},{168,40},{176,48},{184,... | collective-permute-start | bytes 41480 | tf_op jit(solution)/shard_map/ppermute | solution.py:34
  120.6 3.1 %multiply_reduce_fusion.4 = (f32[128]{0:T(128)}, f32[768]{0:T(1024)S(1)}, f32[768]{0:T(1024)S(1)}, bf16[768,128]{1,0:T(8,128)(2,1)}, f32[768,128]{1,0:T(8,128)S(1)}) fusion(f32[12,1,64,128]{3,2,0,1:T(8,128)S(1)} %copy-done, f32[768]{0:T(1024)S(1)} %copy-done.20, f32[768]{0:T(1024)S(1)} %copy-done.21, f32[128]{0:T(128)S(1)} %copy-done.26, ...), kind=kOutput, calls=%fused_computation.126 | convolution fusion | flops 101644672 | bytes 1915904 | tf_op jit(solution)/shard_map/dot_general | solution.py:130
  124.2 4.8 %fusion.40 = f32[1,7,7,128]{3,0,2,1:T(1,128)S(1)} fusion(bf16[1,18,70,128]{3,2,1,0:T(8,128)(2,1)} %get-tuple-element.113, bf16[12,64,1,128]{3,1,0,2:T(8,128)(2,1)S(1)} %bitcast.316), kind=kOutput, calls=%fused_computation.66 | convolution fusion | flops 9633792 | bytes 544256 | tf_op jit(solution)/shard_map/conv_general_dilated | solution.py:58
  134.5 4.8 %all-to-all-start = ((bf16[8,8,34,128]{3,1,2,0:T(8,128)(2,1)}), bf16[8,8,34,128]{3,1,2,0:T(8,128)(2,1)S(1)}, u32[]{:S(2)}, u32[]{:S(2)}) async-start(bf16[8,8,34,128]{3,1,2,0:T(8,128)(2,1)} %copy.440), calls=%async_computation | async-start | bytes 1114112 | tf_op jit(solution)/shard_map/all_to_all | solution.py:157
  141.4 8.7 %collective-permute-start.13 = (bf16[3,64,128]{2,0,1:T(4,128)(2,1)S(1)}, bf16[3,64,128]{2,0,1:T(4,128)(2,1)S(1)}, u32[]{:S(2)}, u32[]{:S(2)}) collective-permute-start(bf16[3,64,128]{2,0,1:T(4,128)(2,1)S(1)} %copy.420), channel_id=1, source_target_pairs={{8,0},{16,8},{24,16},{32,24},{40,32},{48,40},{56,48},{64,56},{72,6... | collective-permute-start | bytes 147464 | tf_op jit(solution)/shard_map/ppermute | solution.py:26
  151.2 2.6 %collective-permute-start.14 = (bf16[18,3,128]{2,0,1:T(8,128)(2,1)S(1)}, bf16[18,3,128]{2,0,1:T(8,128)(2,1)S(1)}, u32[]{:S(2)}, u32[]{:S(2)}) collective-permute-start(bf16[18,3,128]{2,0,1:T(8,128)(2,1)S(1)} %get-tuple-element.109), channel_id=1, source_target_pairs={{384,0},{392,8},{400,16},{408,24},{416,32},{424,40},{432,48},{440,... | collective-permute-start | bytes 41480 | tf_op jit(solution)/shard_map/ppermute | solution.py:34
  153.8 4.8 %collective-permute-start.15 = (bf16[18,3,128]{2,0,1:T(8,128)(2,1)S(1)}, bf16[18,3,128]{2,0,1:T(8,128)(2,1)S(1)}, u32[]{:S(2)}, u32[]{:S(2)}) collective-permute-start(bf16[18,3,128]{2,0,1:T(8,128)(2,1)S(1)} %get-tuple-element.110), channel_id=1, source_target_pairs={{128,0},{136,8},{144,16},{152,24},{160,32},{168,40},{176,48},{184,... | collective-permute-start | bytes 41480 | tf_op jit(solution)/shard_map/ppermute | solution.py:34
  161.9 12.7 %all-to-all-start.1 = ((bf16[8,34,128]{2,1,0:T(8,128)(2,1)}), bf16[8,34,128]{2,1,0:T(8,128)(2,1)S(1)}, u32[]{:S(2)}, u32[]{:S(2)}) async-start(bf16[8,34,128]{2,1,0:T(8,128)(2,1)} %copy.441), calls=%async_computation.1 | async-start | bytes 163840 | tf_op jit(solution)/shard_map/all_to_all | solution.py:157
  176.2 5.7 %all-to-all-done.1 = bf16[8,34,128]{2,1,0:T(8,128)(2,1)S(1)} async-done(((bf16[8,34,128]{2,1,0:T(8,128)(2,1)}), bf16[8,34,128]{2,1,0:T(8,128)(2,1)S(1)}, u32[]{:S(2)}, u32[]{:S(2)}) %all-to-all-start.1) | async-done | bytes 69664 | tf_op jit(solution)/shard_map/all_to_all | solution.py:157
  182.7 5.2 %all-to-all-start.2 = ((bf16[8,34,128]{2,1,0:T(8,128)(2,1)}), bf16[8,34,128]{2,1,0:T(8,128)(2,1)S(1)}, u32[]{:S(2)}, u32[]{:S(2)}) async-start(bf16[8,34,128]{2,1,0:T(8,128)(2,1)} %broadcast_in_dim.93), calls=%async_computation.2 | async-start | bytes 163840 | tf_op jit(solution)/shard_map/all_to_all | solution.py:157
  188.1 7.5 %all-to-all-done.2 = bf16[8,34,128]{2,1,0:T(8,128)(2,1)S(1)} async-done(((bf16[8,34,128]{2,1,0:T(8,128)(2,1)}), bf16[8,34,128]{2,1,0:T(8,128)(2,1)S(1)}, u32[]{:S(2)}, u32[]{:S(2)}) %all-to-all-start.2) | async-done | bytes 69664 | tf_op jit(solution)/shard_map/all_to_all | solution.py:157
  196.3 3.4 %all-to-all-start.3 = ((bf16[8,34,128]{2,1,0:T(8,128)(2,1)}), bf16[8,34,128]{2,1,0:T(8,128)(2,1)S(1)}, u32[]{:S(2)}, u32[]{:S(2)}) async-start(bf16[8,34,128]{2,1,0:T(8,128)(2,1)} %broadcast_in_dim.94), calls=%async_computation.3 | async-start | bytes 163840 | tf_op jit(solution)/shard_map/all_to_all | solution.py:157
  200.5 6.5 %all-to-all-done.3 = bf16[8,34,128]{2,1,0:T(8,128)(2,1)S(1)} async-done(((bf16[8,34,128]{2,1,0:T(8,128)(2,1)}), bf16[8,34,128]{2,1,0:T(8,128)(2,1)S(1)}, u32[]{:S(2)}, u32[]{:S(2)}) %all-to-all-start.3) | async-done | bytes 69664 | tf_op jit(solution)/shard_map/all_to_all | solution.py:157
  (250 shorter events, 79.4 us)
Async XLA Ops:
  0.6 25.6 %copy-start.37 = (f32[2,128]{1,0:T(2,128)S(1)}, f32[2,128]{1,0:T(2,128)}, u32[]{:S(2)}) copy-start(f32[2,128]{1,0:T(2,128)} %param.17) | copy-start | bytes 3076
  1.5 53.6 %copy-start.32 = (pred[12]{0:T(512)(128)(4,1)}, pred[12]{0:T(512)(128)(4,1)S(1)}, u32[]{:S(2)}) copy-start(pred[12]{0:T(512)(128)(4,1)S(1)} %broadcast_compare_fusion) | copy-start | bytes 40
  3.6 13.8 %collective-permute-start = (bf16[3,64,128]{2,1,0:T(8,128)(2,1)S(1)}, bf16[3,64,128]{2,1,0:T(8,128)(2,1)S(1)}, u32[]{:S(2)}, u32[]{:S(2)}) collective-permute-start(bf16[3,64,128]{2,1,0:T(8,128)(2,1)S(1)} %get-tuple-element.127), channel_id=1, source_target_pairs={{0,8},{8,16},{16,24},{24,32},{32,40},{40,48},{48,56},{56,64},{64,7... | collective-permute-start | bytes 147464 | tf_op jit(solution)/shard_map/ppermute | solution.py:25
  8.2 9.2 %collective-permute-start.1 = (bf16[3,64,128]{2,1,0:T(8,128)(2,1)S(1)}, bf16[3,64,128]{2,1,0:T(8,128)(2,1)S(1)}, u32[]{:S(2)}, u32[]{:S(2)}) collective-permute-start(bf16[3,64,128]{2,1,0:T(8,128)(2,1)S(1)} %get-tuple-element.128), channel_id=1, source_target_pairs={{8,0},{16,8},{24,16},{32,24},{40,32},{48,40},{56,48},{64,56},{72,6... | collective-permute-start | bytes 147464 | tf_op jit(solution)/shard_map/ppermute | solution.py:26
  17.3 46.6 %copy-start.27 = (f32[128]{0:T(128)}, f32[128]{0:T(128)S(1)}, u32[]{:S(2)}) copy-start(f32[128]{0:T(128)S(1)} %get-tuple-element.140) | copy-start | bytes 1540
  17.4 8.8 %collective-permute-start.2 = (bf16[18,3,128]{2,1,0:T(4,128)(2,1)S(1)}, bf16[18,3,128]{2,1,0:T(4,128)(2,1)S(1)}, u32[]{:S(2)}, u32[]{:S(2)}) collective-permute-start(bf16[18,3,128]{2,1,0:T(4,128)(2,1)S(1)} %get-tuple-element.119), channel_id=1, source_target_pairs={{384,0},{392,8},{400,16},{408,24},{416,32},{424,40},{432,48},{440,... | collective-permute-start | bytes 41480 | tf_op jit(solution)/shard_map/ppermute | solution.py:34
  19.4 8.5 %collective-permute-start.3 = (bf16[18,3,128]{2,1,0:T(4,128)(2,1)S(1)}, bf16[18,3,128]{2,1,0:T(4,128)(2,1)S(1)}, u32[]{:S(2)}, u32[]{:S(2)}) collective-permute-start(bf16[18,3,128]{2,1,0:T(4,128)(2,1)S(1)} %get-tuple-element.120), channel_id=1, source_target_pairs={{128,0},{136,8},{144,16},{152,24},{160,32},{168,40},{176,48},{184,... | collective-permute-start | bytes 41480 | tf_op jit(solution)/shard_map/ppermute | solution.py:34
  26.2 28.9 %copy-start.31 = (f32[128]{0:T(128)}, f32[128]{0:T(128)S(1)}, u32[]{:S(2)}) copy-start(f32[128]{0:T(128)S(1)} %get-tuple-element.137) | copy-start | bytes 1540
  34.2 9.2 %collective-permute-start.5 = (bf16[3,64,128]{2,1,0:T(8,128)(2,1)S(1)}, bf16[3,64,128]{2,1,0:T(8,128)(2,1)S(1)}, u32[]{:S(2)}, u32[]{:S(2)}) collective-permute-start(bf16[3,64,128]{2,1,0:T(8,128)(2,1)S(1)} %bitcast.347), channel_id=1, source_target_pairs={{8,0},{16,8},{24,16},{32,24},{40,32},{48,40},{56,48},{64,56},{72,6... | collective-permute-start | bytes 147464 | tf_op jit(solution)/shard_map/ppermute | solution.py:26
  41.4 6.3 %collective-permute-start.4 = (bf16[3,64,128]{2,1,0:T(8,128)(2,1)S(1)}, bf16[3,64,128]{2,1,0:T(8,128)(2,1)S(1)}, u32[]{:S(2)}, u32[]{:S(2)}) collective-permute-start(bf16[3,64,128]{2,1,0:T(8,128)(2,1)S(1)} %bitcast.346), channel_id=1, source_target_pairs={{0,8},{8,16},{16,24},{24,32},{32,40},{40,48},{48,56},{56,64},{64,7... | collective-permute-start | bytes 147464 | tf_op jit(solution)/shard_map/ppermute | solution.py:25
  47.7 11.1 %collective-permute-start.6 = (bf16[18,3,128]{2,1,0:T(4,128)(2,1)S(1)}, bf16[18,3,128]{2,1,0:T(4,128)(2,1)S(1)}, u32[]{:S(2)}, u32[]{:S(2)}) collective-permute-start(bf16[18,3,128]{2,1,0:T(4,128)(2,1)S(1)} %get-tuple-element.117), channel_id=1, source_target_pairs={{384,0},{392,8},{400,16},{408,24},{416,32},{424,40},{432,48},{440,... | collective-permute-start | bytes 41480 | tf_op jit(solution)/shard_map/ppermute | solution.py:34
  50.5 8.3 %collective-permute-start.7 = (bf16[18,3,128]{2,1,0:T(4,128)(2,1)S(1)}, bf16[18,3,128]{2,1,0:T(4,128)(2,1)S(1)}, u32[]{:S(2)}, u32[]{:S(2)}) collective-permute-start(bf16[18,3,128]{2,1,0:T(4,128)(2,1)S(1)} %get-tuple-element.118), channel_id=1, source_target_pairs={{128,0},{136,8},{144,16},{152,24},{160,32},{168,40},{176,48},{184,... | collective-permute-start | bytes 41480 | tf_op jit(solution)/shard_map/ppermute | solution.py:34
  71.2 22.2 %collective-permute-start.8 = (bf16[3,64,128]{2,0,1:T(4,128)(2,1)}, bf16[3,64,128]{2,0,1:T(4,128)(2,1)}, u32[]{:S(2)}, u32[]{:S(2)}) collective-permute-start(bf16[3,64,128]{2,0,1:T(4,128)(2,1)} %copy.410), channel_id=1, source_target_pairs={{0,8},{8,16},{16,24},{24,32},{32,40},{40,48},{48,56},{56,64},{64,7... | collective-permute-start | bytes 147464 | tf_op jit(solution)/shard_map/ppermute | solution.py:25
  73.7 19.7 %collective-permute-start.9 = (bf16[3,64,128]{2,0,1:T(4,128)(2,1)}, bf16[3,64,128]{2,0,1:T(4,128)(2,1)}, u32[]{:S(2)}, u32[]{:S(2)}) collective-permute-start(bf16[3,64,128]{2,0,1:T(4,128)(2,1)} %copy.411), channel_id=1, source_target_pairs={{8,0},{16,8},{24,16},{32,24},{40,32},{48,40},{56,48},{64,56},{72,6... | collective-permute-start | bytes 147464 | tf_op jit(solution)/shard_map/ppermute | solution.py:26
  95.5 14.0 %collective-permute-start.10 = (bf16[18,3,128]{2,0,1:T(8,128)(2,1)}, bf16[18,3,128]{2,0,1:T(8,128)(2,1)}, u32[]{:S(2)}, u32[]{:S(2)}) collective-permute-start(bf16[18,3,128]{2,0,1:T(8,128)(2,1)} %get-tuple-element.111), channel_id=1, source_target_pairs={{384,0},{392,8},{400,16},{408,24},{416,32},{424,40},{432,48},{440,... | collective-permute-start | bytes 41480 | tf_op jit(solution)/shard_map/ppermute | solution.py:34
  100.1 9.4 %collective-permute-start.11 = (bf16[18,3,128]{2,0,1:T(8,128)(2,1)}, bf16[18,3,128]{2,0,1:T(8,128)(2,1)}, u32[]{:S(2)}, u32[]{:S(2)}) collective-permute-start(bf16[18,3,128]{2,0,1:T(8,128)(2,1)} %get-tuple-element.112), channel_id=1, source_target_pairs={{128,0},{136,8},{144,16},{152,24},{160,32},{168,40},{176,48},{184,... | collective-permute-start | bytes 41480 | tf_op jit(solution)/shard_map/ppermute | solution.py:34
  134.5 26.6 %all-to-all-start = ((bf16[8,8,34,128]{3,1,2,0:T(8,128)(2,1)}), bf16[8,8,34,128]{3,1,2,0:T(8,128)(2,1)S(1)}, u32[]{:S(2)}, u32[]{:S(2)}) async-start(bf16[8,8,34,128]{3,1,2,0:T(8,128)(2,1)} %copy.440), calls=%async_computation | async-start | bytes 1114112 | tf_op jit(solution)/shard_map/all_to_all | solution.py:157
  139.4 11.7 %collective-permute-start.12 = (bf16[3,64,128]{2,0,1:T(4,128)(2,1)S(1)}, bf16[3,64,128]{2,0,1:T(4,128)(2,1)S(1)}, u32[]{:S(2)}, u32[]{:S(2)}) collective-permute-start(bf16[3,64,128]{2,0,1:T(4,128)(2,1)S(1)} %copy.419), channel_id=1, source_target_pairs={{0,8},{8,16},{16,24},{24,32},{32,40},{40,48},{48,56},{56,64},{64,7... | collective-permute-start | bytes 147464 | tf_op jit(solution)/shard_map/ppermute | solution.py:25
  141.4 9.8 %collective-permute-start.13 = (bf16[3,64,128]{2,0,1:T(4,128)(2,1)S(1)}, bf16[3,64,128]{2,0,1:T(4,128)(2,1)S(1)}, u32[]{:S(2)}, u32[]{:S(2)}) collective-permute-start(bf16[3,64,128]{2,0,1:T(4,128)(2,1)S(1)} %copy.420), channel_id=1, source_target_pairs={{8,0},{16,8},{24,16},{32,24},{40,32},{48,40},{56,48},{64,56},{72,6... | collective-permute-start | bytes 147464 | tf_op jit(solution)/shard_map/ppermute | solution.py:26
  151.2 7.5 %collective-permute-start.14 = (bf16[18,3,128]{2,0,1:T(8,128)(2,1)S(1)}, bf16[18,3,128]{2,0,1:T(8,128)(2,1)S(1)}, u32[]{:S(2)}, u32[]{:S(2)}) collective-permute-start(bf16[18,3,128]{2,0,1:T(8,128)(2,1)S(1)} %get-tuple-element.109), channel_id=1, source_target_pairs={{384,0},{392,8},{400,16},{408,24},{416,32},{424,40},{432,48},{440,... | collective-permute-start | bytes 41480 | tf_op jit(solution)/shard_map/ppermute | solution.py:34
  153.8 6.9 %collective-permute-start.15 = (bf16[18,3,128]{2,0,1:T(8,128)(2,1)S(1)}, bf16[18,3,128]{2,0,1:T(8,128)(2,1)S(1)}, u32[]{:S(2)}, u32[]{:S(2)}) collective-permute-start(bf16[18,3,128]{2,0,1:T(8,128)(2,1)S(1)} %get-tuple-element.110), channel_id=1, source_target_pairs={{128,0},{136,8},{144,16},{152,24},{160,32},{168,40},{176,48},{184,... | collective-permute-start | bytes 41480 | tf_op jit(solution)/shard_map/ppermute | solution.py:34
  161.9 20.1 %all-to-all-start.1 = ((bf16[8,34,128]{2,1,0:T(8,128)(2,1)}), bf16[8,34,128]{2,1,0:T(8,128)(2,1)S(1)}, u32[]{:S(2)}, u32[]{:S(2)}) async-start(bf16[8,34,128]{2,1,0:T(8,128)(2,1)} %copy.441), calls=%async_computation.1 | async-start | bytes 163840 | tf_op jit(solution)/shard_map/all_to_all | solution.py:157
  182.7 12.9 %all-to-all-start.2 = ((bf16[8,34,128]{2,1,0:T(8,128)(2,1)}), bf16[8,34,128]{2,1,0:T(8,128)(2,1)S(1)}, u32[]{:S(2)}, u32[]{:S(2)}) async-start(bf16[8,34,128]{2,1,0:T(8,128)(2,1)} %broadcast_in_dim.93), calls=%async_computation.2 | async-start | bytes 163840 | tf_op jit(solution)/shard_map/all_to_all | solution.py:157
  196.3 10.7 %all-to-all-start.3 = ((bf16[8,34,128]{2,1,0:T(8,128)(2,1)}), bf16[8,34,128]{2,1,0:T(8,128)(2,1)S(1)}, u32[]{:S(2)}, u32[]{:S(2)}) async-start(bf16[8,34,128]{2,1,0:T(8,128)(2,1)} %broadcast_in_dim.94), calls=%async_computation.3 | async-start | bytes 163840 | tf_op jit(solution)/shard_map/all_to_all | solution.py:157
  (38 other events, 158.9 us)

commit v2 on v1

v2 whole, which is shorter than its diff:
```python
import functools
import math

import jax
import jax.numpy as jnp
from jax import lax
from jax.experimental import pallas as pl
from jax.experimental.pallas import tpu as pltpu
from jax.sharding import PartitionSpec as P

KS = 7
TAPS = KS * KS
RIM = KS // 2
WIDE = 2 * RIM
TILE = ("zh", "y", "c")
DP = ("zl", "x")
EDGE = 16
EPSILON = 1e-06
SQRT_HALF = 0.7071067811865476
INV_ROOT_TWO_PI = 0.3989422804014327
F32 = jnp.float32
BF16 = jnp.bfloat16
GAIN_ROW = TAPS
SCALE_ROW = TAPS + 1


def dot(a, b, over=((1,), (0,))):
    return lax.dot_general(a, b, (over, ((), ())), preferred_element_type=F32)


def gelu_parts(preact):
    normal_cdf = 0.5 * (1.0 + lax.erf(preact * SQRT_HALF))
    return (
        preact * normal_cdf,
        normal_cdf + preact * jnp.exp(-0.5 * preact * preact) * INV_ROOT_TWO_PI,
    )


def picker(rows, columns, source_of):
    i = lax.broadcasted_iota(jnp.int32, (rows, columns), 0)
    j = lax.broadcasted_iota(jnp.int32, (rows, columns), 1)
    return jnp.where(j == source_of(i), 1.0, 0.0).astype(BF16)


def row_flag(flip_ref, tile_ref, row, height, width):
    place = tile_ref[0] * height + row
    column = lax.div(place, 3 * width)
    level = lax.div(lax.rem(place, 3 * width), width)
    return jnp.where(flip_ref[4 * level + column] > 0, 1, 0)


def turner(flag, width):
    return picker(width, width, lambda i: i + flag * (width - 1 - 2 * i))


def moments(convolved):
    average = jnp.mean(convolved, axis=-1, keepdims=True)
    centered = convolved - average
    inv_std = lax.rsqrt(jnp.mean(centered * centered, axis=-1, keepdims=True) + EPSILON)
    return centered * inv_std, inv_std


def tap_row(taps, t):
    return jnp.broadcast_to(taps[pl.ds(t, 1), :], (8, taps.shape[1]))


def convolve(source, width, taps, turned, rows, groups, emit):
    def group(q, carry):
        base = pl.multiple_of(q * 8, 8)
        sums = [None] * rows
        centers = [None] * rows
        for j in range(KS):
            weights = [
                tap_row(taps, TAPS - 1 - (KS * i + j) if turned else KS * i + j) for i in range(KS)
            ]
            for r in range(rows + KS - 1):
                cells = source[pl.ds(base + (r * width + j), 8), :]
                if j == RIM and 0 <= r - RIM < rows:
                    centers[r - RIM] = cells
                for i in range(KS):
                    out = r - i
                    if 0 <= out < rows:
                        term = cells * weights[i]
                        sums[out] = term if sums[out] is None else sums[out] + term
            if j == RIM:
                emit(base, centers, None)
        emit(base, None, sums)
        return carry

    lax.fori_loop(0, groups, group, 0)


def tap_sums(source, width, source_start, grad, grad_width, grad_start, rows, groups, out):
    for j in range(KS):

        def group(q, sums, j=j):
            base = pl.multiple_of(q * 8, 8)
            sums = list(sums)
            grads = [
                grad[pl.ds(base + (grad_start + r * grad_width), 8), :] for r in range(rows)
            ]
            for r in range(rows + KS - 1):
                cells = source[pl.ds(base + (source_start + r * width + j), 8), :]
                for i in range(KS):
                    if 0 <= r - i < rows:
                        sums[i] = sums[i] + cells * grads[r - i]
            return tuple(sums)

        zero = jnp.zeros((8, source.shape[1]), F32)
        sums = lax.fori_loop(0, groups, group, (zero,) * KS)
        for i in range(KS):
            out[pl.ds(KS * i + j, 1), :] = jnp.sum(sums[i], axis=0, keepdims=True)


def orient_kernel(height, width, flip, tile, fields, cotangent, canon, up, east, west):
    far = 2 * width
    to_east = picker(
        EDGE,
        far,
        lambda i: jnp.where(
            i < WIDE, width - WIDE + i, jnp.where(i < WIDE + RIM, far - RIM + i - WIDE, -1)
        ),
    )
    to_west = picker(
        EDGE, far, lambda i: jnp.where(i < WIDE, i, jnp.where(i < WIDE + RIM, width + i - WIDE, -1))
    )
    for r in range(height):
        turn = turner(row_flag(flip, tile, r, height, width), width)
        cells = slice(r * width, (r + 1) * width)
        a = dot(turn, fields[cells, :]).astype(BF16)
        b = dot(turn, cotangent[cells, :]).astype(BF16)
        canon[cells, :] = a
        up[cells, :] = b
        both = jnp.concatenate([a, b], axis=0)
        edge = slice(r * EDGE, (r + 1) * EDGE)
        east[edge, :] = dot(to_east, both).astype(BF16)
        west[edge, :] = dot(to_west, both).astype(BF16)


def widen_row(before, own, after, start, halo, width, total):
    def source_of(i):
        return jnp.where(
            i < halo,
            start + i,
            jnp.where(
                i < halo + width,
                EDGE + i - halo,
                jnp.where(i < 2 * halo + width, start + EDGE + i - halo, -1),
            ),
        )

    both = jnp.concatenate([before, own, after], axis=0)
    return dot(picker(total, width + 2 * EDGE, source_of), both).astype(BF16)


def widen_kernel(height, width, before, after, canon, up, canon_x, up_x, to_next, to_prev):
    full, slim = width + 16, width + 8
    for r in range(height):
        edge = slice(r * EDGE, (r + 1) * EDGE)
        cells = slice(r * width, (r + 1) * width)
        a = widen_row(before[edge, :], canon[cells, :], after[edge, :], 0, WIDE, width, full)
        b = widen_row(before[edge, :], up[cells, :], after[edge, :], WIDE, RIM, width, slim)
        canon_x[r * full : (r + 1) * full, :] = a
        up_x[r * slim : (r + 1) * slim, :] = b
        if r < WIDE:
            to_prev[r * full : (r + 1) * full, :] = a
        if r < RIM:
            to_prev[WIDE * full + r * slim : WIDE * full + (r + 1) * slim, :] = b
        if r >= height - WIDE:
            k = r - (height - WIDE)
            to_next[k * full : (k + 1) * full, :] = a
        if r >= height - RIM:
            k = r - (height - RIM)
            to_next[WIDE * full + k * slim : WIDE * full + (k + 1) * slim, :] = b


def widen_grad_kernel(height, width, before, after, grad, grad_x, to_next, to_prev):
    full = width + 16
    for r in range(height):
        edge = slice(r * EDGE, (r + 1) * EDGE)
        cells = slice(r * width, (r + 1) * width)
        a = widen_row(before[edge, :], grad[cells, :], after[edge, :], 0, WIDE, width, full)
        grad_x[r * full : (r + 1) * full, :] = a
        if r < WIDE:
            to_prev[r * full : (r + 1) * full, :] = a
        if r >= height - WIDE:
            k = r - (height - WIDE)
            to_next[k * full : (k + 1) * full, :] = a


def join_rows(target, above, middle, below, count, start):
    rows = middle.shape[0]
    target[0:count, :] = above[start : start + count, :].astype(F32)
    target[count : count + rows, :] = middle[...].astype(F32)
    target[count + rows : 2 * count + rows, :] = below[start : start + count, :].astype(F32)


def forward_kernel(
    height,
    width,
    flip,
    tile,
    above,
    canon_x,
    below,
    up,
    kernel,
    gain,
    weight_in,
    bias,
    weight_out,
    scale,
    result,
    conv0,
    slope0,
    hidden0,
    h1,
    grad_conv,
    east,
    west,
    big,
    bias_sum,
    rows_out,
    x_scratch,
    taps,
    h1_flat,
    middle,
    conv1,
    in_sum,
    out_sum,
):
    full, slim = width + 16, width + 8
    rim_rows = height + 2 * RIM
    join_rows(x_scratch, above, canon_x, below, WIDE * full, 0)
    taps[0:TAPS, :] = kernel[0].astype(F32)

    def emit0(base, centers, sums):
        for r in range(rim_rows):
            if centers is not None:
                h1_flat[pl.ds(base + r * slim, 8), :] = centers[r]
            else:
                conv0[pl.ds(base + r * slim, 8), :] = sums[r]

    convolve(x_scratch, full, taps, False, rim_rows, slim // 8, emit0)

    chunk0 = 2 * slim

    def block0(k, carry):
        cells = pl.ds(pl.multiple_of(k * chunk0, 16), chunk0)
        normed, _ = moments(conv0[cells, :])
        scaled = (normed * gain[0:1, :]).astype(BF16)
        preact = dot(scaled, weight_in[0]) + bias[0:1, :]
        value, slope = gelu_parts(preact)
        hidden = value.astype(BF16)
        slope0[cells, :] = slope.astype(BF16)
        hidden0[cells, :] = hidden
        branch = dot(hidden, weight_out[0])
        state = (h1_flat[cells, :] + scale[0:1, :] * branch).astype(BF16)
        h1[cells, :] = state
        h1_flat[cells, :] = state.astype(F32)
        return carry

    lax.fori_loop(0, rim_rows // 2, block0, 0)

    taps[0:TAPS, :] = kernel[1].astype(F32)

    def emit1(base, centers, sums):
        for r in range(height):
            if centers is not None:
                middle[pl.ds(base + r * width, 8), :] = centers[r]
            else:
                conv1[pl.ds(base + r * width, 8), :] = sums[r]

    convolve(h1_flat, slim, taps, False, height, width // 8, emit1)

    in_sum[...] = jnp.zeros_like(in_sum)
    out_sum[...] = jnp.zeros_like(out_sum)
    bias_sum[...] = jnp.zeros_like(bias_sum)
    rows_out[...] = jnp.zeros_like(rows_out)
    chunk_rows = 3
    chunk1 = chunk_rows * width
    ones = jnp.ones((8, chunk1), BF16)
    to_east = picker(EDGE, width, lambda i: jnp.where(i < WIDE, width - WIDE + i, -1))
    to_west = picker(EDGE, width, lambda i: jnp.where(i < WIDE, i, -1))

    def block1(k, carry):
        cells = pl.ds(pl.multiple_of(k * chunk1, 8), chunk1)
        normed, inv_std = moments(conv1[cells, :])
        gain_row = gain[1:2, :]
        scaled = (normed * gain_row).astype(BF16)
        preact = dot(scaled, weight_in[1]) + bias[1:2, :]
        value, slope = gelu_parts(preact)
        hidden = value.astype(BF16)
        branch = dot(hidden, weight_out[1])
        scale_row = scale[1:2, :]
        state = (middle[cells, :] + scale_row * branch).astype(BF16)
        upstream = up[cells, :]
        grad_branch = (upstream.astype(F32) * scale_row).astype(BF16)
        out_sum[...] += dot(upstream, hidden, ((0,), (0,)))
        grad_preact = (dot(grad_branch, weight_out[1], ((1,), (1,))) * slope).astype(BF16)
        bias_sum[...] += dot(ones, grad_preact)
        in_sum[...] += dot(scaled, grad_preact, ((0,), (0,)))
        grad_scaled = dot(grad_preact, weight_in[1], ((1,), (1,)))
        rows_out[GAIN_ROW : GAIN_ROW + 1, :] += jnp.sum(
            grad_scaled * normed, axis=0, keepdims=True
        )
        e = grad_scaled * gain_row
        grad = inv_std * (
            e
            - jnp.mean(e, axis=-1, keepdims=True)
            - normed * jnp.mean(e * normed, axis=-1, keepdims=True)
        )
        grad = grad.astype(BF16)
        grad_conv[cells, :] = grad
        for r in range(chunk_rows):
            row = k * chunk_rows + r
            turn = turner(row_flag(flip, tile, row, height, width), width)
            own = slice(r * width, (r + 1) * width)
            result[pl.ds(pl.multiple_of(row * width, 8), width), :] = dot(turn, state[own]).astype(
                BF16
            )
            edge = pl.ds(pl.multiple_of(row * EDGE, 8), EDGE)
            east[edge, :] = dot(to_east, grad[own]).astype(BF16)
            west[edge, :] = dot(to_west, grad[own]).astype(BF16)
        return carry

    lax.fori_loop(0, height // chunk_rows, block1, 0)
    pack_weights(in_sum, out_sum, weight_out[1], scale[1:2, :], big, 0, rows_out)


def pack_weights(in_sum, out_sum, weight_out, scale_row, big, first, rows_out):
    channels = in_sum.shape[0]
    members = big.shape[0]
    part = channels // members
    products = out_sum[...].T
    rows_out[SCALE_ROW : SCALE_ROW + 1, :] = jnp.sum(
        products * weight_out.astype(F32), axis=0, keepdims=True
    )
    outward = products * scale_row
    strips = in_sum.shape[1] // channels
    share = outward.shape[0] // members
    piece = share // strips
    for d in range(members):
        for s in range(strips):
            big[d, first + s, 0:part, :] = in_sum[
                d * part : (d + 1) * part, s * channels : (s + 1) * channels
            ].astype(BF16)
            begin = d * share + s * piece
            big[d, first + s, part : part + piece, :] = outward[begin : begin + piece, :].astype(
                BF16
            )


def taps_kernel(height, width, h1, grad_conv, out, source, grad):
    slim = width + 8
    source[...] = h1[...].astype(F32)
    grad[...] = grad_conv[...].astype(F32)
    tap_sums(source, slim, 0, grad, width, 0, height, width // 8, out)


def backward_kernel(
    height,
    width,
    flip,
    tile,
    above,
    grad_x,
    below,
    x_above,
    canon_x,
    x_below,
    up_x,
    kernel,
    gain,
    weight_in,
    weight_out,
    scale,
    conv0,
    slope0,
    hidden0,
    big1,
    bias1,
    rows1,
    taps1,
    grad_input,
    packed,
    g_scratch,
    taps,
    up_flat,
    d_flat,
    g0_flat,
    in_sum,
    out_sum,
    bias_sum,
    rows_all,
):
    full, slim = width + 16, width + 8
    rim_rows = height + 2 * RIM
    channels = gain.shape[1]
    join_rows(g_scratch, above, grad_x, below, WIDE * full, 0)
    join_rows(up_flat, x_above, up_x, x_below, RIM * slim, WIDE * full)
    taps[0:TAPS, :] = kernel[1].astype(F32)

    def emit1(base, centers, sums):
        if sums is not None:
            for r in range(rim_rows):
                cells = pl.ds(base + r * slim, 8)
                d_flat[cells, :] = (up_flat[cells, :] + sums[r]).astype(BF16).astype(F32)

    convolve(g_scratch, full, taps, True, rim_rows, slim // 8, emit1)

    in_sum[...] = jnp.zeros_like(in_sum)
    out_sum[...] = jnp.zeros_like(out_sum)
    bias_sum[...] = jnp.zeros_like(bias_sum)
    rows_all[...] = jnp.zeros_like(rows_all)
    half = rows1.shape[0]
    chunk = 2 * slim

    def owned(k, shape, dim):
        place = lax.broadcasted_iota(jnp.int32, shape, dim)
        second = jnp.where(place >= slim, 1, 0)
        row = 2 * k + second
        column = place - slim * second
        inside = (
            (row >= RIM) & (row < RIM + height) & (column >= RIM) & (column < RIM + width)
        )
        return jnp.where(inside, 1.0, 0.0)

    def block0(k, carry):
        cells = pl.ds(pl.multiple_of(k * chunk, 16), chunk)
        mask = owned(k, (chunk, channels), 0)
        normed, inv_std = moments(conv0[cells, :])
        gain_row = gain[0:1, :]
        scaled = (normed * gain_row * mask).astype(BF16)
        upstream = d_flat[cells, :]
        grad_branch = (upstream * scale[0:1, :]).astype(BF16)
        out_sum[...] += dot((upstream * mask).astype(BF16), hidden0[cells, :], ((0,), (0,)))
        grad_preact = (
            dot(grad_branch, weight_out[0], ((1,), (1,))) * slope0[cells, :].astype(F32)
        ).astype(BF16)
        bias_sum[...] += dot(owned(k, (8, chunk), 1).astype(BF16), grad_preact)
        in_sum[...] += dot(scaled, grad_preact, ((0,), (0,)))
        grad_scaled = dot(grad_preact, weight_in[0], ((1,), (1,)))
        rows_all[GAIN_ROW : GAIN_ROW + 1, :] += jnp.sum(
            grad_scaled * normed * mask, axis=0, keepdims=True
        )
        e = grad_scaled * gain_row
        grad = inv_std * (
            e
            - jnp.mean(e, axis=-1, keepdims=True)
            - normed * jnp.mean(e * normed, axis=-1, keepdims=True)
        )
        g0_flat[cells, :] = grad.astype(BF16).astype(F32)
        return carry

    lax.fori_loop(0, rim_rows // 2, block0, 0)

    taps[0:TAPS, :] = kernel[0].astype(F32)

    def emit0(base, centers, sums):
        if sums is not None:
            for r in range(height):
                own = d_flat[pl.ds(base + ((r + RIM) * slim + RIM), 8), :]
                up_flat[pl.ds(base + r * width, 8), :] = own + sums[r]

    convolve(g0_flat, slim, taps, True, height, width // 8, emit0)
    for r in range(height):
        turn = turner(row_flag(flip, tile, r, height, width), width)
        cells = slice(r * width, (r + 1) * width)
        grad_input[cells, :] = dot(turn, up_flat[cells, :].astype(BF16)).astype(BF16)

    join_rows(g_scratch, x_above, canon_x, x_below, WIDE * full, 0)
    tap_sums(
        g_scratch,
        full,
        RIM * full + RIM,
        g0_flat,
        slim,
        RIM * slim + RIM,
        height,
        width // 8,
        rows_all,
    )
    strips = big1.shape[1]
    pack_weights(in_sum, out_sum, weight_out[0], scale[0:1, :], packed, 0, rows_all)
    big_rows = big1.shape[2]
    packed[:, strips:, 0:big_rows, :] = big1[...]
    rows_all[half:, :] = rows1[...]
    rows_all[half : half + TAPS, :] = taps1[0:TAPS, :]
    small = rows_all[...].T
    members = packed.shape[0]
    part = channels // members
    zeros = jnp.zeros((8, channels), BF16)
    for d in range(members):
        for y in range(2 * strips):
            if y < part // 8:
                begin = d * part + 8 * y
                rows = small[begin : begin + 8, :].astype(BF16)
            elif y < part // 8 + 2:
                sums = bias_sum if y == part // 8 else bias1
                lane = (d // 2) * channels
                rows = sums[:, lane : lane + channels]
                if d % 2:
                    rows = pltpu.roll(rows, channels // 2, 1)
                rows = rows.astype(BF16)
            else:
                rows = zeros
            packed[d, y, big_rows : big_rows + 8, :] = rows


def shape_of(*sizes, dtype=BF16):
    return jax.ShapeDtypeStruct(sizes, dtype)


def call(body, outs, flags=0, ins=0, scratch=(), cost=None):
    smem = pl.BlockSpec(memory_space=pltpu.SMEM)
    vmem = pl.BlockSpec(memory_space=pltpu.VMEM)
    return pl.pallas_call(
        body,
        out_shape=outs,
        in_specs=[smem] * flags + [vmem] * ins,
        out_specs=[vmem] * len(outs),
        scratch_shapes=[pltpu.VMEM(s, F32) for s in scratch],
        cost_estimate=cost,
    )


def shifted(block, axis, distance):
    count = lax.axis_size(axis)
    return lax.ppermute(block, axis, [(i, (i + distance) % count) for i in range(count)])


def exchanged(blocks, axis):
    return lax.all_to_all(blocks, axis, 0, 0, tiled=True)


def summed_shares(packed, hidden):
    members, rows, _, channels = packed.shape
    part = channels // members
    layers = 2
    strips = rows // layers
    share = jnp.sum(exchanged(packed, DP).astype(F32), axis=0)
    piece = jnp.sum(exchanged(share.astype(BF16), "y").astype(F32), axis=0)
    others = lax.axis_size("zh") * lax.axis_size("c")
    copies = jnp.broadcast_to(piece.astype(BF16)[None], (others, *piece.shape))
    piece = jnp.sum(exchanged(copies, ("zh", "c")).astype(F32), axis=0)
    copies = jnp.broadcast_to(piece.astype(BF16)[None], (rows, *piece.shape))
    return exchanged(copies, "y")


def unpacked(full, normalizer, hidden, members):
    rows, _, channels = full.shape
    layers = 2
    strips = rows // layers
    part = channels // members
    piece = hidden // members // strips
    full = full.astype(F32) * normalizer
    inward = full[:, :part].reshape(layers, strips, part, channels)
    outward = full[:, part : part + piece].reshape(layers, -1, channels)
    rest = full[:, part + piece :]
    small = rest[: part // 8].reshape(part, layers, channels // layers).transpose(1, 2, 0)
    bias = rest[part // 8 : part // 8 + layers, 0, : hidden // members]
    return (
        small[:, :TAPS],
        small[:, GAIN_ROW],
        inward.transpose(0, 2, 1, 3).reshape(layers, part, hidden),
        bias,
        outward,
        small[:, SCALE_ROW],
    )


def on_device(
    fields, cotangent, face_flip, kernel, ln_gain, weight_in, bias_in, weight_out, layer_scale
):
    height, width, channels = fields.shape[1:]
    hidden = weight_in.shape[2]
    members = lax.axis_size(DP)
    own, full, slim = height * width, width + 16, width + 8
    rim_rows = height + 2 * RIM
    rim = rim_rows * slim
    tall = (height + 2 * WIDE) * full
    sent = WIDE * full + RIM * slim
    strips = hidden // channels
    big_rows = channels // members + hidden // members // strips
    tile = lax.axis_index(TILE).astype(jnp.int32).reshape(1)

    cells = shape_of(own, channels)
    edges = shape_of(height * EDGE, channels)
    canon, up, east, west = call(
        functools.partial(orient_kernel, height, width), [cells, cells, edges, edges], 2, 2
    )(face_flip, tile, fields.reshape(own, channels), cotangent.reshape(own, channels))
    before = shifted(east, "zh", 1)
    after = shifted(west, "zh", -1)
    canon_x, up_x, to_next, to_prev = call(
        functools.partial(widen_kernel, height, width),
        [
            shape_of(height * full, channels),
            shape_of(height * slim, channels),
            shape_of(sent, channels),
            shape_of(sent, channels),
        ],
        0,
        4,
    )(before, after, canon, up)
    above = shifted(to_next, TILE, 1)
    below = shifted(to_prev, TILE, -1)
    sums = (channels, hidden)
    (
        result,
        conv0,
        slope0,
        hidden0,
        h1,
        grad_conv,
        east,
        west,
        big1,
        bias1,
        rows1,
    ) = call(
        functools.partial(forward_kernel, height, width),
        [
            cells,
            shape_of(rim, channels, dtype=F32),
            shape_of(rim, hidden),
            shape_of(rim, hidden),
            shape_of(rim, channels),
            cells,
            edges,
            edges,
            shape_of(members, strips, big_rows, channels),
            shape_of(8, hidden, dtype=F32),
            shape_of(64, channels, dtype=F32),
        ],
        2,
        10,
        [
            (tall, channels),
            (56, channels),
            (rim, channels),
            (own, channels),
            (own, channels),
            sums,
            sums,
        ],
    )(
        face_flip,
        tile,
        above,
        canon_x,
        below,
        up,
        kernel,
        ln_gain,
        weight_in,
        bias_in,
        weight_out,
        layer_scale,
    )
    before = shifted(east, "zh", 1)
    after = shifted(west, "zh", -1)
    (taps1,) = call(
        functools.partial(taps_kernel, height, width),
        [shape_of(56, channels, dtype=F32)],
        0,
        2,
        [(rim, channels), (own, channels)],
        pl.CostEstimate(flops=2 * TAPS * own * channels, bytes_accessed=1 << 20, transcendentals=0),
    )(h1, grad_conv)
    grad_x, to_next, to_prev = call(
        functools.partial(widen_grad_kernel, height, width),
        [
            shape_of(height * full, channels),
            shape_of(WIDE * full, channels),
            shape_of(WIDE * full, channels),
        ],
        0,
        3,
    )(before, after, grad_conv)
    grad_above = shifted(to_next, TILE, 1)
    grad_below = shifted(to_prev, TILE, -1)
    grad_input, packed = call(
        functools.partial(backward_kernel, height, width),
        [cells, shape_of(members, 2 * strips, big_rows + 8, channels)],
        2,
        19,
        [
            (tall, channels),
            (56, channels),
            (rim, channels),
            (rim, channels),
            (rim, channels),
            sums,
            sums,
            (8, hidden),
            (128, channels),
        ],
    )(
        face_flip,
        tile,
        grad_above,
        grad_x,
        grad_below,
        above,
        canon_x,
        below,
        up_x,
        kernel,
        ln_gain,
        weight_in,
        weight_out,
        layer_scale,
        conv0,
        slope0,
        hidden0,
        big1,
        bias1,
        rows1,
        taps1,
    )
    normalizer = 1.0 / math.sqrt(members * 12 * width * width)
    shares = unpacked(summed_shares(packed, hidden), normalizer, hidden, members)
    return (result.reshape(fields.shape), grad_input.reshape(fields.shape), *shares)


def solution(mesh, sizes=(4, 8, 2, 2, 4)):
    mesh = jax.sharding.Mesh(mesh.devices.reshape(sizes), ("zh", "y", "c", "zl", "x"))
    return jax.shard_map(
        on_device,
        mesh=mesh,
        in_specs=(P(DP, TILE, None, None), P(DP, TILE, None, None)) + (P(),) * 7,
        out_specs=(
            P(DP, TILE, None, None),
            P(DP, TILE, None, None),
            P(None, None, DP),
            P(None, DP),
            P(None, DP, None),
            P(None, DP),
            P(None, DP, None),
            P(None, DP),
        ),
        check_vma=False,
    )
```

time: 214 us -> 152 us (0.71); the launches traced: 211 us -> 152 us
  starting transfers between devices: 99.5 us -> 35.1 us
  blocking collectives: 0 us -> 53.6 us
  Pallas kernels: 0 us -> 44.2 us
  matrix products: 33.9 us -> 0 us
  local copies, waits for them, and re-layouts: 32.6 us -> 7.9 us
  waiting for transfers between devices: 27.6 us -> 9.83 us
  other arithmetic: 15.9 us -> 0.14 us
    all_to_all x0 -> x4, blocking collectives: none -> 53.6 us  [exchanged(): return lax.all_to_all(blocks, axis, 0, 0, tiled=True)]
    pallas_call x0 -> x6, Pallas kernels: none -> 44.2 us  [the longest x1 16.9 us: on_device(): call(functools.partial(forward_kernel, height, width), [cells, shape_of(r...]
    ppermute x16 -> x8, starting transfers between devices: 73.4 us -> 35.1 us  [shifted(): lax.ppermute(block, axis, [(i, (i + distance) % count) for i in range(cou...]
    all_to_all x4 -> x0, starting transfers between devices: 26.1 us -> none  [exchanged(): return lax.all_to_all(blocks, axis, 0, 0, tiled=True)]
    all_to_all x4 -> x0, waiting for transfers between devices: 19.7 us -> none  [exchanged(): return lax.all_to_all(blocks, axis, 0, 0, tiled=True)]
    dot_general x12 -> x0, matrix products: 17.7 us -> none  [the longest x2 4.97 us: backward_block(): jnp.dot(grad_preact, weight_in_row.T, preferred_element_type=jnp.float32)]
    conv_general_dilated x6 -> x0, matrix products: 16.2 us -> none  [the longest x2 9.36 us: tap_sums(): lax.conv_general_dilated(padded[None], grad_conv[:, :, None, :], (1, 1),...]
    convert_element_type x9 -> x0, other arithmetic: 6.8 us -> none  [the longest x2 3.26 us: backward_block(): grad_preact = (jnp.dot(grad_branch, weight_out_row.T, preferred_element_t...]
  transfers between devices with their start and end apart: 20 -> 8, of which waited for: 6 -> 3; matrix products, arithmetic and copies ran while one was open for 13% -> 1% of each run, Pallas kernels for 0% -> 2%
where the time goes in v2:
time: 152 us
  blocking collectives  53.6 us (35%)
  Pallas kernels  44.2 us (29%)
  starting transfers between devices  35.1 us (23%)
  waiting for transfers between devices  9.83 us (6%)
  local copies, waits for them, and re-layouts  7.9 us (5%)
    all_to_all x4, blocking collectives, exchanged(): return lax.all_to_all(blocks, axis, 0, 0, tiled=True)  53.6 us
    ppermute x8, starting transfers between devices, shifted(): lax.ppermute(block, axis, [(i, (i + distance) % count) for i in range(cou...  35.1 us
    pallas_call x1, Pallas kernels, on_device(): call(functools.partial(forward_kernel, height, width), [cells, shape_of(r...  16.9 us
    pallas_call x1, Pallas kernels, on_device(): call(functools.partial(backward_kernel, height, width), [cells, shape_of(...  16.1 us
    ppermute x8, waiting for transfers between devices, shifted(): lax.ppermute(block, axis, [(i, (i + distance) % count) for i in range(cou...  9.83 us
    unnamed x18, local copies, waits for them, and re-layouts  4.57 us
    pallas_call x1, Pallas kernels, on_device(): call(functools.partial(orient_kernel, height, width), [cells, cells, edge...  3.49 us
    pallas_call x1, Pallas kernels, on_device(): call(functools.partial(taps_kernel, height, width), [shape_of(56, channel...  3.32 us
  transfers between devices with their start and end apart: 8, of which 3 were waited for; matrix products, arithmetic and copies ran while one was open for 1% of the time, Pallas kernels for 2%

profile of v2, /device:TPU:1, one launch (start us, length us, event | category | flops | bytes accessed | tf_op | source)
XLA Modules:
  0.0 151.7 jit_solution(17855106475355738458)
XLA Ops:
  0.6 3.5 %shard_map.152 = (bf16[768,128]{1,0:T(8,128)(2,1)}, bf16[768,128]{1,0:T(8,128)(2,1)}, bf16[192,128]{1,0:T(8,128)(2,1)}, bf16[192,128]{1,0:T(8,128)(2,1)}) custom-call(s32[12]{0:T(128)} %flip.5, s32[1]{0:T(128)} %bitcast.tile, bf16[768,128]{1,0:T(8,128)(2,1)} %bitcast.21, bf16[768,128]{1,0:T(8,128)(2,1)} %bitcast.22), custom_call_target="tpu_custom_call" | custom-call | tf_op jit(solution)/shard_map/pallas_call | solution.py:590
  4.1 6.6 %collective-permute-start = (bf16[192,128]{1,0:T(8,128)(2,1)}, bf16[192,128]{1,0:T(8,128)(2,1)S(1)}, u32[]{:S(2)}, u32[]{:S(2)}) collective-permute-start(bf16[192,128]{1,0:T(8,128)(2,1)} %get-tuple-element.32), channel_id=1, source_target_pairs={{0,128},{128,256},{256,384},{384,0},{1,129},{129,257},{257,385},{3... | collective-permute-start | bytes 147464 | tf_op jit(solution)/shard_map/ppermute | solution.py:530
  10.8 6.8 %collective-permute-start.1 = (bf16[192,128]{1,0:T(8,128)(2,1)}, bf16[192,128]{1,0:T(8,128)(2,1)S(1)}, u32[]{:S(2)}, u32[]{:S(2)}) collective-permute-start(bf16[192,128]{1,0:T(8,128)(2,1)} %get-tuple-element.33), channel_id=1, source_target_pairs={{0,384},{128,0},{256,128},{384,256},{1,385},{129,1},{257,129},{385... | collective-permute-start | bytes 147464 | tf_op jit(solution)/shard_map/ppermute | solution.py:530
  17.6 1.9 %collective-permute-done.1.after = bf16[192,128]{1,0:T(8,128)(2,1)S(1)} collective-permute-done((bf16[192,128]{1,0:T(8,128)(2,1)}, bf16[192,128]{1,0:T(8,128)(2,1)S(1)}, u32[]{:S(2)}, u32[]{:S(2)}) %collective-permute-start.1) | collective-permute-done | bytes 49184 | tf_op jit(solution)/shard_map/ppermute | solution.py:530
  20.1 2.3 %shard_map.153 = (bf16[960,128]{1,0:T(8,128)(2,1)}, bf16[864,128]{1,0:T(8,128)(2,1)}, bf16[696,128]{1,0:T(8,128)(2,1)}, bf16[696,128]{1,0:T(8,128)(2,1)}) custom-call(bf16[192,128]{1,0:T(8,128)(2,1)} %copy-done.6, bf16[192,128]{1,0:T(8,128)(2,1)} %copy-done.7, bf16[768,128]{1,0:T(8,128)(2,1)} %get-tuple-element.34.canon, bf16[768,128]{1,0:T(8,128)(2,1)} %get-tuple-element.35.up), custom_call_target="tpu_custom_call" | custom-call | tf_op jit(solution)/shard_map/pallas_call | solution.py:595
  22.4 5.2 %collective-permute-start.2 = (bf16[696,128]{1,0:T(8,128)(2,1)}, bf16[696,128]{1,0:T(8,128)(2,1)S(1)}, u32[]{:S(2)}, u32[]{:S(2)}) collective-permute-start(bf16[696,128]{1,0:T(8,128)(2,1)} %get-tuple-element.36), channel_id=1, source_target_pairs={{0,8},{8,16},{16,24},{24,32},{32,40},{40,48},{48,56},{56,64},{64,7... | collective-permute-start | bytes 534536 | tf_op jit(solution)/shard_map/ppermute | solution.py:530
  27.6 1.9 %collective-permute-start.3 = (bf16[696,128]{1,0:T(8,128)(2,1)}, bf16[696,128]{1,0:T(8,128)(2,1)S(1)}, u32[]{:S(2)}, u32[]{:S(2)}) collective-permute-start(bf16[696,128]{1,0:T(8,128)(2,1)} %get-tuple-element.38), channel_id=1, source_target_pairs={{0,504},{8,0},{16,8},{24,16},{32,24},{40,32},{48,40},{56,48},{64,5... | collective-permute-start | bytes 534536 | tf_op jit(solution)/shard_map/ppermute | solution.py:530
  29.5 1.4 copy.35.kernel
  30.9 4.0 %collective-permute-done.3.below.x_below = bf16[696,128]{1,0:T(8,128)(2,1)S(1)} collective-permute-done((bf16[696,128]{1,0:T(8,128)(2,1)}, bf16[696,128]{1,0:T(8,128)(2,1)S(1)}, u32[]{:S(2)}, u32[]{:S(2)}) %collective-permute-start.3) | collective-permute-done | bytes 178208 | tf_op jit(solution)/shard_map/ppermute | solution.py:530
  34.9 0.7 copy-done.1
  35.6 16.9 %shard_map.154 = (bf16[768,128]{1,0:T(8,128)(2,1)}, f32[1296,128]{1,0:T(8,128)}, bf16[1296,512]{1,0:T(8,128)(2,1)}, bf16[1296,512]{1,0:T(8,128)(2,1)}, bf16[1296...) custom-call(s32[12]{0:T(128)} %flip.5, ...), custom_call_target="tpu_custom_call" | custom-call | tf_op jit(solution)/shard_map/pallas_call | solution.py:621
  52.5 5.4 %collective-permute-start.4 = (bf16[192,128]{1,0:T(8,128)(2,1)}, bf16[192,128]{1,0:T(8,128)(2,1)S(1)}, u32[]{:S(2)}, u32[]{:S(2)}) collective-permute-start(bf16[192,128]{1,0:T(8,128)(2,1)} %get-tuple-element.40), channel_id=1, source_target_pairs={{0,128},{128,256},{256,384},{384,0},{1,129},{129,257},{257,385},{3... | collective-permute-start | bytes 147464 | tf_op jit(solution)/shard_map/ppermute | solution.py:530
  57.9 2.0 %collective-permute-start.5 = (bf16[192,128]{1,0:T(8,128)(2,1)}, bf16[192,128]{1,0:T(8,128)(2,1)S(1)}, u32[]{:S(2)}, u32[]{:S(2)}) collective-permute-start(bf16[192,128]{1,0:T(8,128)(2,1)} %get-tuple-element.41), channel_id=1, source_target_pairs={{0,384},{128,0},{256,128},{384,256},{1,385},{129,1},{257,129},{385... | collective-permute-start | bytes 147464 | tf_op jit(solution)/shard_map/ppermute | solution.py:530
  59.9 3.9 %collective-permute-done.5.after = bf16[192,128]{1,0:T(8,128)(2,1)S(1)} collective-permute-done((bf16[192,128]{1,0:T(8,128)(2,1)}, bf16[192,128]{1,0:T(8,128)(2,1)S(1)}, u32[]{:S(2)}, u32[]{:S(2)}) %collective-permute-start.5) | collective-permute-done | bytes 49184 | tf_op jit(solution)/shard_map/ppermute | solution.py:530
  64.4 2.1 %shard_map.155 = (bf16[960,128]{1,0:T(8,128)(2,1)}, bf16[480,128]{1,0:T(8,128)(2,1)}, bf16[480,128]{1,0:T(8,128)(2,1)}) custom-call(bf16[192,128]{1,0:T(8,128)(2,1)} %copy-done.4, bf16[192,128]{1,0:T(8,128)(2,1)} %copy-done.5, bf16[768,128]{1,0:T(8,128)(2,1)} %get-tuple-element.42.grad.grad_conv), custom_call_target="tpu_custom_call" | custom-call | tf_op jit(solution)/shard_map/pallas_call | solution.py:671
  66.5 3.3 %collective-permute-start.6 = (bf16[480,128]{1,0:T(8,128)(2,1)}, bf16[480,128]{1,0:T(8,128)(2,1)S(1)}, u32[]{:S(2)}, u32[]{:S(2)}) collective-permute-start(bf16[480,128]{1,0:T(8,128)(2,1)} %get-tuple-element.43), channel_id=1, source_target_pairs={{0,8},{8,16},{16,24},{24,32},{32,40},{40,48},{48,56},{56,64},{64,7... | collective-permute-start | bytes 368648 | tf_op jit(solution)/shard_map/ppermute | solution.py:530
  69.8 3.9 %collective-permute-start.7 = (bf16[480,128]{1,0:T(8,128)(2,1)}, bf16[480,128]{1,0:T(8,128)(2,1)S(1)}, u32[]{:S(2)}, u32[]{:S(2)}) collective-permute-start(bf16[480,128]{1,0:T(8,128)(2,1)} %get-tuple-element.45), channel_id=1, source_target_pairs={{0,504},{8,0},{16,8},{24,16},{32,24},{40,32},{48,40},{56,48},{64,5... | collective-permute-start | bytes 368648 | tf_op jit(solution)/shard_map/ppermute | solution.py:530
  73.8 3.3 %shard_map.156.taps1 = f32[56,128]{1,0:T(8,128)} custom-call(bf16[1296,128]{1,0:T(8,128)(2,1)} %get-tuple-element.53.h1, bf16[768,128]{1,0:T(8,128)(2,1)} %get-tuple-element.42.grad.grad_conv), custom_call_target="tpu_custom_call" | custom-call | flops 9633792 | bytes 1048576 | tf_op jit(solution)/shard_map/pallas_call | solution.py:663
  77.8 16.1 %shard_map.157 = (bf16[768,128]{1,0:T(8,128)(2,1)}, bf16[8,8,40,128]{3,2,1,0:T(8,128)(2,1)}) custom-call(s32[12]{0:T(128)} %flip.5, s32[1]{0:T(128)} %bitcast.tile, bf16[480,128]{1,0:T(8,128)(2,1)} %copy-done.2, bf16[960,128]{1,0:T(8,128)(2,1)} %get-tuple-element.44.grad_x, bf16[480,128]{1,0:T(8,128)(2,1)} %copy-done.3, bf16[696,128]{1,0:T(8,128)(2,1)} %copy-done, ...), custom_call_target="tpu_custom_call" | custom-call | tf_op jit(solution)/shard_map/pallas_call | solution.py:683
  93.9 13.0 %all_to_all.20 = bf16[8,8,40,128]{3,2,1,0:T(8,128)(2,1)S(1)} all-to-all(bf16[8,8,40,128]{3,2,1,0:T(8,128)(2,1)} %get-tuple-element.55), channel_id=1, replica_groups=mesh['zh'=4,'y'=8,'c'=2,'zl'=2,'x'=4] {'zl','x'}, dimensions={0} | all-to-all | bytes 1310720 | tf_op jit(solution)/shard_map/all_to_all | solution.py:534
  107.0 19.6 %all_to_all.21 = bf16[8,40,128]{2,1,0:T(8,128)(2,1)S(1)} all-to-all(bf16[8,40,128]{2,1,0:T(8,128)(2,1)S(1)} %reduce_sum.36), channel_id=1, replica_groups=mesh['zh'=4,'y'=8,'c'=2,'zl'=2,'x'=4] {'y'}, dimensions={0} | all-to-all | bytes 163840 | tf_op jit(solution)/shard_map/all_to_all | solution.py:534
  126.7 11.2 %all_to_all.22 = bf16[8,40,128]{2,1,0:T(8,128)(2,1)S(1)} all-to-all(bf16[8,40,128]{2,1,0:T(8,128)(2,1)S(1)} %broadcast_in_dim.4), channel_id=1, replica_groups=mesh['zh'=4,'y'=8,'c'=2,'zl'=2,'x'=4] {'zh','c'}, dimensions={0} | all-to-all | bytes 163840 | tf_op jit(solution)/shard_map/all_to_all | solution.py:534
  137.9 9.9 %all_to_all.23 = bf16[8,40,128]{2,1,0:T(8,128)(2,1)S(1)} all-to-all(bf16[8,40,128]{2,1,0:T(8,128)(2,1)S(1)} %broadcast_in_dim.5), channel_id=1, replica_groups=mesh['zh'=4,'y'=8,'c'=2,'zl'=2,'x'=4] {'y'}, dimensions={0} | all-to-all | bytes 163840 | tf_op jit(solution)/shard_map/all_to_all | solution.py:534
  150.4 0.6 copy.39
  (34 shorter events, 5.4 us)
Async XLA Ops:
  4.1 13.4 %collective-permute-start = (bf16[192,128]{1,0:T(8,128)(2,1)}, bf16[192,128]{1,0:T(8,128)(2,1)S(1)}, u32[]{:S(2)}, u32[]{:S(2)}) collective-permute-start(bf16[192,128]{1,0:T(8,128)(2,1)} %get-tuple-element.32), channel_id=1, source_target_pairs={{0,128},{128,256},{256,384},{384,0},{1,129},{129,257},{257,385},{3... | collective-permute-start | bytes 147464 | tf_op jit(solution)/shard_map/ppermute | solution.py:530
  10.8 8.7 %collective-permute-start.1 = (bf16[192,128]{1,0:T(8,128)(2,1)}, bf16[192,128]{1,0:T(8,128)(2,1)S(1)}, u32[]{:S(2)}, u32[]{:S(2)}) collective-permute-start(bf16[192,128]{1,0:T(8,128)(2,1)} %get-tuple-element.33), channel_id=1, source_target_pairs={{0,384},{128,0},{256,128},{384,256},{1,385},{129,1},{257,129},{385... | collective-permute-start | bytes 147464 | tf_op jit(solution)/shard_map/ppermute | solution.py:530
  17.5 1.9 %copy-start.6 = (bf16[192,128]{1,0:T(8,128)(2,1)}, bf16[192,128]{1,0:T(8,128)(2,1)S(1)}, u32[]{:S(2)}) copy-start(bf16[192,128]{1,0:T(8,128)(2,1)S(1)} %collective-permute-done.before) | copy-start | bytes 147460
  19.5 0.6 copy-start.7
  22.4 8.5 %collective-permute-start.2 = (bf16[696,128]{1,0:T(8,128)(2,1)}, bf16[696,128]{1,0:T(8,128)(2,1)S(1)}, u32[]{:S(2)}, u32[]{:S(2)}) collective-permute-start(bf16[696,128]{1,0:T(8,128)(2,1)} %get-tuple-element.36), channel_id=1, source_target_pairs={{0,8},{8,16},{16,24},{24,32},{32,40},{40,48},{48,56},{56,64},{64,7... | collective-permute-start | bytes 534536 | tf_op jit(solution)/shard_map/ppermute | solution.py:530
  27.6 7.3 %collective-permute-start.3 = (bf16[696,128]{1,0:T(8,128)(2,1)}, bf16[696,128]{1,0:T(8,128)(2,1)S(1)}, u32[]{:S(2)}, u32[]{:S(2)}) collective-permute-start(bf16[696,128]{1,0:T(8,128)(2,1)} %get-tuple-element.38), channel_id=1, source_target_pairs={{0,504},{8,0},{16,8},{24,16},{32,24},{40,32},{48,40},{56,48},{64,5... | collective-permute-start | bytes 534536 | tf_op jit(solution)/shard_map/ppermute | solution.py:530
  30.9 4.0 %copy-start = (bf16[696,128]{1,0:T(8,128)(2,1)}, bf16[696,128]{1,0:T(8,128)(2,1)S(1)}, u32[]{:S(2)}) copy-start(bf16[696,128]{1,0:T(8,128)(2,1)S(1)} %collective-permute-done.2.above.x_above) | copy-start | bytes 534532
  34.9 0.7 copy-start.1
  52.5 7.4 %collective-permute-start.4 = (bf16[192,128]{1,0:T(8,128)(2,1)}, bf16[192,128]{1,0:T(8,128)(2,1)S(1)}, u32[]{:S(2)}, u32[]{:S(2)}) collective-permute-start(bf16[192,128]{1,0:T(8,128)(2,1)} %get-tuple-element.40), channel_id=1, source_target_pairs={{0,128},{128,256},{256,384},{384,0},{1,129},{129,257},{257,385},{3... | collective-permute-start | bytes 147464 | tf_op jit(solution)/shard_map/ppermute | solution.py:530
  57.9 5.9 %collective-permute-start.5 = (bf16[192,128]{1,0:T(8,128)(2,1)}, bf16[192,128]{1,0:T(8,128)(2,1)S(1)}, u32[]{:S(2)}, u32[]{:S(2)}) collective-permute-start(bf16[192,128]{1,0:T(8,128)(2,1)} %get-tuple-element.41), channel_id=1, source_target_pairs={{0,384},{128,0},{256,128},{384,256},{1,385},{129,1},{257,129},{385... | collective-permute-start | bytes 147464 | tf_op jit(solution)/shard_map/ppermute | solution.py:530
  59.9 3.9 %copy-start.4 = (bf16[192,128]{1,0:T(8,128)(2,1)}, bf16[192,128]{1,0:T(8,128)(2,1)S(1)}, u32[]{:S(2)}) copy-start(bf16[192,128]{1,0:T(8,128)(2,1)S(1)} %collective-permute-done.4.before) | copy-start | bytes 147460
  63.8 0.6 copy-start.5
  66.5 10.6 %collective-permute-start.6 = (bf16[480,128]{1,0:T(8,128)(2,1)}, bf16[480,128]{1,0:T(8,128)(2,1)S(1)}, u32[]{:S(2)}, u32[]{:S(2)}) collective-permute-start(bf16[480,128]{1,0:T(8,128)(2,1)} %get-tuple-element.43), channel_id=1, source_target_pairs={{0,8},{8,16},{16,24},{24,32},{32,40},{40,48},{48,56},{56,64},{64,7... | collective-permute-start | bytes 368648 | tf_op jit(solution)/shard_map/ppermute | solution.py:530
  69.8 7.3 %collective-permute-start.7 = (bf16[480,128]{1,0:T(8,128)(2,1)}, bf16[480,128]{1,0:T(8,128)(2,1)S(1)}, u32[]{:S(2)}, u32[]{:S(2)}) collective-permute-start(bf16[480,128]{1,0:T(8,128)(2,1)} %get-tuple-element.45), channel_id=1, source_target_pairs={{0,504},{8,0},{16,8},{24,16},{32,24},{40,32},{48,40},{56,48},{64,5... | collective-permute-start | bytes 368648 | tf_op jit(solution)/shard_map/ppermute | solution.py:530
  77.1 0.7 copy-start.2
  77.1 0.7 copy-start.3

commit v3 on v2

--- a/solution.py
+++ b/solution.py
@@ -15,6 +15,7 @@
 TILE = ("zh", "y", "c")
 DP = ("zl", "x")
 EDGE = 16
+LIMIT = 24 << 20
 EPSILON = 1e-06
 SQRT_HALF = 0.7071067811865476
 INV_ROOT_TWO_PI = 0.3989422804014327
@@ -112,29 +113,47 @@
             out[pl.ds(KS * i + j, 1), :] = jnp.sum(sums[i], axis=0, keepdims=True)
 
 
-def orient_kernel(height, width, flip, tile, fields, cotangent, canon, up, east, west):
+def edge_kernel(height, width, flip, tile, fields, cotangent, east, west):
     far = 2 * width
-    to_east = picker(
-        EDGE,
-        far,
-        lambda i: jnp.where(
-            i < WIDE, width - WIDE + i, jnp.where(i < WIDE + RIM, far - RIM + i - WIDE, -1)
-        ),
-    )
-    to_west = picker(
-        EDGE, far, lambda i: jnp.where(i < WIDE, i, jnp.where(i < WIDE + RIM, width + i - WIDE, -1))
-    )
+
+    def turned(flag, i):
+        return jnp.where(
+            i >= width, width + i - width + flag * (3 * width - 1 - 2 * i), i + flag * (width - 1 - 2 * i)
+        )
+
+    def east_of(flag, i):
+        place = jnp.where(i < WIDE, width - WIDE + i, far - RIM + i - WIDE)
+        return jnp.where(i < WIDE + RIM, turned(flag, place), -1)
+
+    def west_of(flag, i):
+        place = jnp.where(i < WIDE, i, width + i - WIDE)
+        return jnp.where(i < WIDE + RIM, turned(flag, place), -1)
+
+    picks = []
+    for flag in (0, 1):
+        to_east = picker(EDGE, far, functools.partial(east_of, flag)).astype(F32)
+        to_west = picker(EDGE, far, functools.partial(west_of, flag)).astype(F32)
+        picks.append(jnp.concatenate([to_east, to_west], axis=0))
     for r in range(height):
-        turn = turner(row_flag(flip, tile, r, height, width), width)
+        flag = row_flag(flip, tile, r, height, width)
         cells = slice(r * width, (r + 1) * width)
-        a = dot(turn, fields[cells, :]).astype(BF16)
-        b = dot(turn, cotangent[cells, :]).astype(BF16)
-        canon[cells, :] = a
-        up[cells, :] = b
-        both = jnp.concatenate([a, b], axis=0)
+        both = jnp.concatenate([fields[cells, :], cotangent[cells, :]], axis=0)
+        pick = jnp.where(flag > 0, picks[1], picks[0]).astype(BF16)
+        edges = dot(pick, both).astype(BF16)
         edge = slice(r * EDGE, (r + 1) * EDGE)
-        east[edge, :] = dot(to_east, both).astype(BF16)
-        west[edge, :] = dot(to_west, both).astype(BF16)
+        east[edge, :] = edges[:EDGE]
+        west[edge, :] = edges[EDGE:]
+
+
+def orient_kernel(height, width, flip, tile, fields, cotangent, canon, up):
+    plain = turner(0, width).astype(F32)
+    flipped = turner(1, width).astype(F32)
+    for r in range(height):
+        flag = row_flag(flip, tile, r, height, width)
+        turn = jnp.where(flag > 0, flipped, plain).astype(BF16)
+        cells = slice(r * width, (r + 1) * width)
+        canon[cells, :] = dot(turn, fields[cells, :]).astype(BF16)
+        up[cells, :] = dot(turn, cotangent[cells, :]).astype(BF16)
 
 
 def widen_row(before, own, after, start, halo, width, total):
@@ -218,16 +237,15 @@
     grad_conv,
     east,
     west,
-    big,
-    bias_sum,
-    rows_out,
+    scaled1,
+    hidden1,
+    grad_preact1,
+    gain_sum,
     x_scratch,
     taps,
     h1_flat,
     middle,
     conv1,
-    in_sum,
-    out_sum,
 ):
     full, slim = width + 16, width + 8
     rim_rows = height + 2 * RIM
@@ -273,13 +291,9 @@
 
     convolve(h1_flat, slim, taps, False, height, width // 8, emit1)
 
-    in_sum[...] = jnp.zeros_like(in_sum)
-    out_sum[...] = jnp.zeros_like(out_sum)
-    bias_sum[...] = jnp.zeros_like(bias_sum)
-    rows_out[...] = jnp.zeros_like(rows_out)
+    gain_sum[...] = jnp.zeros_like(gain_sum)
     chunk_rows = 3
     chunk1 = chunk_rows * width
-    ones = jnp.ones((8, chunk1), BF16)
     to_east = picker(EDGE, width, lambda i: jnp.where(i < WIDE, width - WIDE + i, -1))
     to_west = picker(EDGE, width, lambda i: jnp.where(i < WIDE, i, -1))
 
@@ -296,12 +310,12 @@
         state = (middle[cells, :] + scale_row * branch).astype(BF16)
         upstream = up[cells, :]
         grad_branch = (upstream.astype(F32) * scale_row).astype(BF16)
-        out_sum[...] += dot(upstream, hidden, ((0,), (0,)))
         grad_preact = (dot(grad_branch, weight_out[1], ((1,), (1,))) * slope).astype(BF16)
-        bias_sum[...] += dot(ones, grad_preact)
-        in_sum[...] += dot(scaled, grad_preact, ((0,), (0,)))
+        scaled1[cells, :] = scaled
+        hidden1[cells, :] = hidden
+        grad_preact1[cells, :] = grad_preact
         grad_scaled = dot(grad_preact, weight_in[1], ((1,), (1,)))
-        rows_out[GAIN_ROW : GAIN_ROW + 1, :] += jnp.sum(
+        gain_sum[0:1, :] += jnp.sum(
             grad_scaled * normed, axis=0, keepdims=True
         )
         e = grad_scaled * gain_row
@@ -325,6 +339,28 @@
         return carry
 
     lax.fori_loop(0, height // chunk_rows, block1, 0)
+
+
+def weights_kernel(
+    scaled, hidden, grad_preact, up, gain_sum, weight_out, scale, big, bias_sum, rows_out, in_sum, out_sum
+):
+    in_sum[...] = jnp.zeros_like(in_sum)
+    out_sum[...] = jnp.zeros_like(out_sum)
+    bias_sum[...] = jnp.zeros_like(bias_sum)
+    rows_out[...] = jnp.zeros_like(rows_out)
+    steps = 3
+    chunk = scaled.shape[0] // steps
+    ones = jnp.ones((8, chunk), BF16)
+
+    def step(k, carry):
+        cells = pl.ds(pl.multiple_of(k * chunk, 8), chunk)
+        out_sum[...] += dot(up[cells, :], hidden[cells, :], ((0,), (0,)))
+        bias_sum[...] += dot(ones, grad_preact[cells, :])
+        in_sum[...] += dot(scaled[cells, :], grad_preact[cells, :], ((0,), (0,)))
+        return carry
+
+    lax.fori_loop(0, steps, step, 0)
+    rows_out[GAIN_ROW : GAIN_ROW + 1, :] = gain_sum[0:1, :]
     pack_weights(in_sum, out_sum, weight_out[1], scale[1:2, :], big, 0, rows_out)
 
 
@@ -361,8 +397,6 @@
 def backward_kernel(
     height,
     width,
-    flip,
-    tile,
     above,
     grad_x,
     below,
@@ -382,7 +416,8 @@
     bias1,
     rows1,
     taps1,
-    grad_input,
+    d1,
+    grad0,
     packed,
     g_scratch,
     taps,
@@ -450,24 +485,13 @@
             - jnp.mean(e, axis=-1, keepdims=True)
             - normed * jnp.mean(e * normed, axis=-1, keepdims=True)
         )
-        g0_flat[cells, :] = grad.astype(BF16).astype(F32)
+        grad = grad.astype(BF16)
+        grad0[cells, :] = grad
+        g0_flat[cells, :] = grad.astype(F32)
+        d1[cells, :] = upstream.astype(BF16)
         return carry
 
     lax.fori_loop(0, rim_rows // 2, block0, 0)
-
-    taps[0:TAPS, :] = kernel[0].astype(F32)
-
-    def emit0(base, centers, sums):
-        if sums is not None:
-            for r in range(height):
-                own = d_flat[pl.ds(base + ((r + RIM) * slim + RIM), 8), :]
-                up_flat[pl.ds(base + r * width, 8), :] = own + sums[r]
-
-    convolve(g0_flat, slim, taps, True, height, width // 8, emit0)
-    for r in range(height):
-        turn = turner(row_flag(flip, tile, r, height, width), width)
-        cells = slice(r * width, (r + 1) * width)
-        grad_input[cells, :] = dot(turn, up_flat[cells, :].astype(BF16)).astype(BF16)
 
     join_rows(g_scratch, x_above, canon_x, x_below, WIDE * full, 0)
     tap_sums(
@@ -508,6 +532,53 @@
             packed[d, y, big_rows : big_rows + 8, :] = rows
 
 
+def spread_kernel(height, width, flip, tile, kernel, d1, grad0, grad_input, taps, g_flat, d_flat, out):
+    slim = width + 8
+    taps[0:TAPS, :] = kernel[0].astype(F32)
+    g_flat[...] = grad0[...].astype(F32)
+    d_flat[...] = d1[...].astype(F32)
+
+    def emit(base, centers, sums):
+        if sums is not None:
+            for r in range(height):
+                own = d_flat[pl.ds(base + ((r + RIM) * slim + RIM), 8), :]
+                out[pl.ds(base + r * width, 8), :] = own + sums[r]
+
+    convolve(g_flat, slim, taps, True, height, width // 8, emit)
+    plain = turner(0, width).astype(F32)
+    flipped = turner(1, width).astype(F32)
+    for r in range(height):
+        turn = jnp.where(row_flag(flip, tile, r, height, width) > 0, flipped, plain).astype(BF16)
+        cells = slice(r * width, (r + 1) * width)
+        grad_input[cells, :] = dot(turn, out[cells, :].astype(BF16)).astype(BF16)
+
+
+def unpack_kernel(
+    normalizer, full, tap_rows, gain_row, inward, bias, outward, scale_row
+):
+    layers, part, hidden = inward.shape
+    channels = full.shape[2]
+    strips = hidden // channels
+    piece = outward.shape[1] // strips
+    begin = part + piece
+    for b in range(layers):
+        for s in range(strips):
+            block = full[b * strips + s, 0:begin, :].astype(F32) * normalizer
+            inward[b, :, s * channels : (s + 1) * channels] = block[:part]
+            outward[b, s * piece : (s + 1) * piece, :] = block[part:]
+    chunks = part // 8
+    small = jnp.concatenate([full[y, begin : begin + 8, :] for y in range(chunks)], axis=0)
+    across = small.astype(F32) * normalizer
+    small = across.T
+    half = channels // layers
+    for b in range(layers):
+        tap_rows[b] = across[:, b * half : b * half + TAPS]
+        gain_row[b : b + 1, :] = small[b * half + GAIN_ROW : b * half + GAIN_ROW + 1]
+        scale_row[b : b + 1, :] = small[b * half + SCALE_ROW : b * half + SCALE_ROW + 1]
+        rows = full[chunks + b, begin : begin + 8, :].astype(F32) * normalizer
+        bias[b : b + 1, :] = rows[0:1, : bias.shape[1]]
+
+
 def shape_of(*sizes, dtype=BF16):
     return jax.ShapeDtypeStruct(sizes, dtype)
 
@@ -522,7 +593,12 @@
         out_specs=[vmem] * len(outs),
         scratch_shapes=[pltpu.VMEM(s, F32) for s in scratch],
         cost_estimate=cost,
+        compiler_params=pltpu.CompilerParams(vmem_limit_bytes=LIMIT),
     )
+
+
+def work(flops):
+    return pl.CostEstimate(flops=flops, bytes_accessed=1 << 20, transcendentals=0)
 
 
 def shifted(block, axis, distance):
@@ -549,25 +625,24 @@
 
 
 def unpacked(full, normalizer, hidden, members):
-    rows, _, channels = full.shape
+    channels = full.shape[2]
     layers = 2
-    strips = rows // layers
     part = channels // members
-    piece = hidden // members // strips
-    full = full.astype(F32) * normalizer
-    inward = full[:, :part].reshape(layers, strips, part, channels)
-    outward = full[:, part : part + piece].reshape(layers, -1, channels)
-    rest = full[:, part + piece :]
-    small = rest[: part // 8].reshape(part, layers, channels // layers).transpose(1, 2, 0)
-    bias = rest[part // 8 : part // 8 + layers, 0, : hidden // members]
-    return (
-        small[:, :TAPS],
-        small[:, GAIN_ROW],
-        inward.transpose(0, 2, 1, 3).reshape(layers, part, hidden),
-        bias,
-        outward,
-        small[:, SCALE_ROW],
-    )
+    row = shape_of(layers, part, dtype=F32)
+    taps, *others = call(
+        functools.partial(unpack_kernel, normalizer),
+        [
+            shape_of(layers, part, TAPS, dtype=F32),
+            row,
+            shape_of(layers, part, hidden, dtype=F32),
+            shape_of(layers, hidden // members, dtype=F32),
+            shape_of(layers, hidden // members, channels, dtype=F32),
+            row,
+        ],
+        0,
+        1,
+    )(full)
+    return (taps.transpose(0, 2, 1), *others)
 
 
 def on_device(
@@ -587,9 +662,11 @@
 
     cells = shape_of(own, channels)
     edges = shape_of(height * EDGE, channels)
-    canon, up, east, west = call(
-        functools.partial(orient_kernel, height, width), [cells, cells, edges, edges], 2, 2
-    )(face_flip, tile, fields.reshape(own, channels), cotangent.reshape(own, channels))
+    given = (face_flip, tile, fields.reshape(own, channels), cotangent.reshape(own, channels))
+    east, west = call(functools.partial(edge_kernel, height, width), [edges, edges], 2, 2)(*given)
+    canon, up = call(
+        functools.partial(orient_kernel, height, width), [cells, cells], 2, 2, cost=work(own * 1024)
+    )(*given)
     before = shifted(east, "zh", 1)
     after = shifted(west, "zh", -1)
     canon_x, up_x, to_next, to_prev = call(
@@ -615,9 +692,10 @@
         grad_conv,
         east,
         west,
-        big1,
-        bias1,
-        rows1,
+        scaled1,
+        hidden1,
+        grad_preact1,
+        gain1,
     ) = call(
         functools.partial(forward_kernel, height, width),
         [
@@ -629,9 +707,10 @@
             cells,
             edges,
             edges,
-            shape_of(members, strips, big_rows, channels),
-            shape_of(8, hidden, dtype=F32),
-            shape_of(64, channels, dtype=F32),
+            cells,
+            shape_of(own, hidden),
+            shape_of(own, hidden),
+            shape_of(8, channels, dtype=F32),
         ],
         2,
         10,
@@ -641,8 +720,6 @@
             (rim, channels),
             (own, channels),
             (own, channels),
-            sums,
-            sums,
         ],
     )(
         face_flip,
@@ -660,13 +737,26 @@
     )
     before = shifted(east, "zh", 1)
     after = shifted(west, "zh", -1)
+    big1, bias1, rows1 = call(
+        weights_kernel,
+        [
+            shape_of(members, strips, big_rows, channels),
+            shape_of(8, hidden, dtype=F32),
+            shape_of(64, channels, dtype=F32),
+        ],
+        0,
+        7,
+        [sums, sums],
+        work(4 * own * hidden * channels),
+    )(scaled1, hidden1, grad_preact1, up, gain1, weight_out, layer_scale)
+    due, big1 = lax.optimization_barrier((grad_conv, big1))
     (taps1,) = call(
         functools.partial(taps_kernel, height, width),
         [shape_of(56, channels, dtype=F32)],
         0,
         2,
         [(rim, channels), (own, channels)],
-        pl.CostEstimate(flops=2 * TAPS * own * channels, bytes_accessed=1 << 20, transcendentals=0),
+        work(2 * TAPS * own * channels),
     )(h1, grad_conv)
     grad_x, to_next, to_prev = call(
         functools.partial(widen_grad_kernel, height, width),
@@ -677,13 +767,17 @@
         ],
         0,
         3,
-    )(before, after, grad_conv)
+    )(before, after, due)
     grad_above = shifted(to_next, TILE, 1)
     grad_below = shifted(to_prev, TILE, -1)
-    grad_input, packed = call(
+    d1, grad0, packed = call(
         functools.partial(backward_kernel, height, width),
-        [cells, shape_of(members, 2 * strips, big_rows + 8, channels)],
-        2,
+        [
+            shape_of(rim, channels),
+            shape_of(rim, channels),
+            shape_of(members, 2 * strips, big_rows + 8, channels),
+        ],
+        0,
         19,
         [
             (tall, channels),
@@ -697,8 +791,6 @@
             (128, channels),
         ],
     )(
-        face_flip,
-        tile,
         grad_above,
         grad_x,
         grad_below,
@@ -719,6 +811,14 @@
         rows1,
         taps1,
     )
+    (grad_input,) = call(
+        functools.partial(spread_kernel, height, width),
+        [cells],
+        2,
+        3,
+        [(56, channels), (rim, channels), (rim, channels), (own, channels)],
+        work(2 * TAPS * own * channels),
+    )(face_flip, tile, kernel, d1, grad0)
     normalizer = 1.0 / math.sqrt(members * 12 * width * width)
     shares = unpacked(summed_shares(packed, hidden), normalizer, hidden, members)
     return (result.reshape(fields.shape), grad_input.reshape(fields.shape), *shares)

time: 152 us -> 135 us (0.89)
  Pallas kernels: 44.2 us -> 34 us
  blocking collectives: 53.6 us -> 44.6 us
  local copies, waits for them, and re-layouts: 7.9 us -> 4 us
  starting transfers between devices: 35.1 us -> 38.5 us
  waiting for transfers between devices: 9.83 us -> 12.5 us
    all_to_all x4 -> x3, blocking collectives: 53.6 us -> 44.6 us  [exchanged(): return lax.all_to_all(blocks, axis, 0, 0, tiled=True)]
    all_to_all x0 -> x1, waiting for transfers between devices: none -> 4.08 us  [exchanged(): return lax.all_to_all(blocks, axis, 0, 0, tiled=True)]
    all_to_all x0 -> x1, starting transfers between devices: none -> 3.36 us  [exchanged(): return lax.all_to_all(blocks, axis, 0, 0, tiled=True)]
    slice x6 -> x0, local copies, waits for them, and re-layouts: 2.59 us -> none  [the longest x2 0.74 us: unpacked(): small[:, SCALE_ROW]]
    pallas_call x1, Pallas kernels: 16.9 us -> 14.4 us  [on_device(): call(functools.partial(forward_kernel, height, width), [cells, shape_of(r...]
    pallas_call x2 -> x6, Pallas kernels: 19.6 us -> 17.3 us  [the longest x1 10.6 us: on_device(): call(functools.partial(backward_kernel, height, width), [shape_of(rim, ch...]
    pallas_call x1, Pallas kernels: 2.31 us -> 0.4 us  [on_device(): call(functools.partial(widen_kernel, height, width), [shape_of(height * f...]
    pallas_call x1, Pallas kernels: 2.07 us -> 0.28 us  [on_device(): call(functools.partial(widen_grad_kernel, height, width), [shape_of(heigh...]
  transfers between devices with their start and end apart: 8 -> 9, of which waited for: 3 -> 5; matrix products, arithmetic and copies ran while one was open for 1% -> 1% of each run, Pallas kernels for 2% -> 5%
where the time goes in v3:
time: 135 us
  blocking collectives  44.6 us (33%)
  starting transfers between devices  38.5 us (29%)
  Pallas kernels  34 us (25%)
  waiting for transfers between devices  12.5 us (9%)
  local copies, waits for them, and re-layouts  4 us (3%)
    all_to_all x3, blocking collectives, exchanged(): return lax.all_to_all(blocks, axis, 0, 0, tiled=True)  44.6 us
    ppermute x8, starting transfers between devices, shifted(): lax.ppermute(block, axis, [(i, (i + distance) % count) for i in range(cou...  35.1 us
    pallas_call x1, Pallas kernels, on_device(): call(functools.partial(forward_kernel, height, width), [cells, shape_of(r...  14.4 us
    pallas_call x1, Pallas kernels, on_device(): call(functools.partial(backward_kernel, height, width), [shape_of(rim, ch...  10.6 us
    ppermute x8, waiting for transfers between devices, shifted(): lax.ppermute(block, axis, [(i, (i + distance) % count) for i in range(cou...  8.39 us
    all_to_all x1, waiting for transfers between devices, exchanged(): return lax.all_to_all(blocks, axis, 0, 0, tiled=True)  4.08 us
    all_to_all x1, starting transfers between devices, exchanged(): return lax.all_to_all(blocks, axis, 0, 0, tiled=True)  3.36 us
    unnamed x19, local copies, waits for them, and re-layouts  3.33 us
  transfers between devices with their start and end apart: 9, of which 5 were waited for; matrix products, arithmetic and copies ran while one was open for 1% of the time, Pallas kernels for 5%

profile of v3, /device:TPU:1, one launch (start us, length us, event | category | flops | bytes accessed | tf_op | source)
XLA Modules:
  0.0 134.6 jit_solution(18434937420712750109)
XLA Ops:
  0.7 1.0 copy-done.2
  1.6 0.9 copy-done.3
  4.0 6.6 %collective-permute-start = (bf16[192,128]{1,0:T(8,128)(2,1)S(1)}, bf16[192,128]{1,0:T(8,128)(2,1)S(1)}, u32[]{:S(2)}, u32[]{:S(2)}) collective-permute-start(bf16[192,128]{1,0:T(8,128)(2,1)S(1)} %get-tuple-element.45), channel_id=1, source_target_pairs={{0,128},{128,256},{256,384},{384,0},{1,129},{129,257},{257,385},{3... | collective-permute-start | bytes 147464 | tf_op jit(solution)/shard_map/ppermute | solution.py:606
  10.6 6.8 %collective-permute-start.1 = (bf16[192,128]{1,0:T(8,128)(2,1)S(1)}, bf16[192,128]{1,0:T(8,128)(2,1)S(1)}, u32[]{:S(2)}, u32[]{:S(2)}) collective-permute-start(bf16[192,128]{1,0:T(8,128)(2,1)S(1)} %get-tuple-element.46), channel_id=1, source_target_pairs={{0,384},{128,0},{256,128},{384,256},{1,385},{129,1},{257,129},{385... | collective-permute-start | bytes 147464 | tf_op jit(solution)/shard_map/ppermute | solution.py:606
  17.4 0.8 shard_map.153
  18.2 0.9 collective-permute-done.1.after
  19.5 5.2 %collective-permute-start.2 = (bf16[696,128]{1,0:T(8,128)(2,1)S(1)}, bf16[696,128]{1,0:T(8,128)(2,1)S(1)}, u32[]{:S(2)}, u32[]{:S(2)}) collective-permute-start(bf16[696,128]{1,0:T(8,128)(2,1)S(1)} %get-tuple-element.49), channel_id=1, source_target_pairs={{0,8},{8,16},{16,24},{24,32},{32,40},{40,48},{48,56},{56,64},{64,7... | collective-permute-start | bytes 534536 | tf_op jit(solution)/shard_map/ppermute | solution.py:606
  24.8 1.9 %collective-permute-start.3 = (bf16[696,128]{1,0:T(8,128)(2,1)S(1)}, bf16[696,128]{1,0:T(8,128)(2,1)S(1)}, u32[]{:S(2)}, u32[]{:S(2)}) collective-permute-start(bf16[696,128]{1,0:T(8,128)(2,1)S(1)} %get-tuple-element.51), channel_id=1, source_target_pairs={{0,504},{8,0},{16,8},{24,16},{32,24},{40,32},{48,40},{56,48},{64,5... | collective-permute-start | bytes 534536 | tf_op jit(solution)/shard_map/ppermute | solution.py:606
  27.4 4.4 %collective-permute-done.3.below.x_below = bf16[696,128]{1,0:T(8,128)(2,1)S(1)} collective-permute-done((bf16[696,128]{1,0:T(8,128)(2,1)S(1)}, bf16[696,128]{1,0:T(8,128)(2,1)S(1)}, u32[]{:S(2)}, u32[]{:S(2)}) %collective-permute-start.3) | collective-permute-done | bytes 178208 | tf_op jit(solution)/shard_map/ppermute | solution.py:606
  31.9 14.4 %shard_map.155 = (bf16[768,128]{1,0:T(8,128)(2,1)}, f32[1296,128]{1,0:T(8,128)S(1)}, bf16[1296,512]{1,0:T(8,128)(2,1)S(1)}, bf16[1296,512]{1,0:T(8,128)(2,1)S(1)...) custom-call(s32[12]{0:T(128)S(1)} %copy-done.5, ...), custom_call_target="tpu_custom_call" | custom-call | tf_op jit(solution)/shard_map/pallas_call | solution.py:699
  46.2 5.4 %collective-permute-start.4 = (bf16[192,128]{1,0:T(8,128)(2,1)S(1)}, bf16[192,128]{1,0:T(8,128)(2,1)S(1)}, u32[]{:S(2)}, u32[]{:S(2)}) collective-permute-start(bf16[192,128]{1,0:T(8,128)(2,1)S(1)} %get-tuple-element.53), channel_id=1, source_target_pairs={{0,128},{128,256},{256,384},{384,0},{1,129},{129,257},{257,385},{3... | collective-permute-start | bytes 147464 | tf_op jit(solution)/shard_map/ppermute | solution.py:606
  51.6 2.0 %collective-permute-start.5 = (bf16[192,128]{1,0:T(8,128)(2,1)S(1)}, bf16[192,128]{1,0:T(8,128)(2,1)S(1)}, u32[]{:S(2)}, u32[]{:S(2)}) collective-permute-start(bf16[192,128]{1,0:T(8,128)(2,1)S(1)} %get-tuple-element.54), channel_id=1, source_target_pairs={{0,384},{128,0},{256,128},{384,256},{1,385},{129,1},{257,129},{385... | collective-permute-start | bytes 147464 | tf_op jit(solution)/shard_map/ppermute | solution.py:606
  53.6 1.1 shard_map.156
  54.7 2.6 %collective-permute-done.5.after = bf16[192,128]{1,0:T(8,128)(2,1)S(1)} collective-permute-done((bf16[192,128]{1,0:T(8,128)(2,1)S(1)}, bf16[192,128]{1,0:T(8,128)(2,1)S(1)}, u32[]{:S(2)}, u32[]{:S(2)}) %collective-permute-start.5) | collective-permute-done | bytes 49184 | tf_op jit(solution)/shard_map/ppermute | solution.py:606
  57.6 3.2 %collective-permute-start.6 = (bf16[480,128]{1,0:T(8,128)(2,1)S(1)}, bf16[480,128]{1,0:T(8,128)(2,1)S(1)}, u32[]{:S(2)}, u32[]{:S(2)}) collective-permute-start(bf16[480,128]{1,0:T(8,128)(2,1)S(1)} %get-tuple-element.62), channel_id=1, source_target_pairs={{0,8},{8,16},{16,24},{24,32},{32,40},{40,48},{48,56},{56,64},{64,7... | collective-permute-start | bytes 368648 | tf_op jit(solution)/shard_map/ppermute | solution.py:606
  60.8 4.0 %collective-permute-start.7 = (bf16[480,128]{1,0:T(8,128)(2,1)S(1)}, bf16[480,128]{1,0:T(8,128)(2,1)S(1)}, u32[]{:S(2)}, u32[]{:S(2)}) collective-permute-start(bf16[480,128]{1,0:T(8,128)(2,1)S(1)} %get-tuple-element.64), channel_id=1, source_target_pairs={{0,504},{8,0},{16,8},{24,16},{32,24},{40,32},{48,40},{56,48},{64,5... | collective-permute-start | bytes 368648 | tf_op jit(solution)/shard_map/ppermute | solution.py:606
  64.9 1.7 %shard_map.158.taps1 = f32[56,128]{1,0:T(8,128)S(1)} custom-call(bf16[1296,128]{1,0:T(8,128)(2,1)S(1)} %get-tuple-element.72.h1, bf16[768,128]{1,0:T(8,128)(2,1)S(1)} %get-tuple-element.61.grad.grad_conv), custom_call_target="tpu_custom_call" | custom-call | flops 9633792 | bytes 1048576 | tf_op jit(solution)/shard_map/pallas_call | solution.py:753
  67.0 10.6 %shard_map.159 = (bf16[1296,128]{1,0:T(8,128)(2,1)S(1)}, bf16[1296,128]{1,0:T(8,128)(2,1)S(1)}, bf16[8,8,40,128]{3,2,1,0:T(8,128)(2,1)S(1)}) custom-call(bf16[480,128]{1,0:T(8,128)(2,1)S(1)} %collective-permute-done.6.above, bf16[960,128]{1,0:T(8,128)(2,1)S(1)} %get-tuple-element.63.grad_x, bf16[480,128]{1,0:T(8,128)(2,1)S(1)} %collective-permute-done.7.below, ...), custom_call_target="tpu_custom_call" | custom-call | tf_op jit(solution)/shard_map/pallas_call | solution.py:773
  77.6 13.1 %all_to_all.20 = bf16[8,8,40,128]{3,2,1,0:T(8,128)(2,1)S(1)} all-to-all(bf16[8,8,40,128]{3,2,1,0:T(8,128)(2,1)S(1)} %get-tuple-element.75), channel_id=1, replica_groups=mesh['zh'=4,'y'=8,'c'=2,'zl'=2,'x'=4] {'zl','x'}, dimensions={0} | all-to-all | bytes 1310720 | tf_op jit(solution)/shard_map/all_to_all | solution.py:610
  90.8 20.2 %all_to_all.21 = bf16[8,40,128]{2,1,0:T(8,128)(2,1)S(1)} all-to-all(bf16[8,40,128]{2,1,0:T(8,128)(2,1)S(1)} %reduce_sum.36), channel_id=1, replica_groups=mesh['zh'=4,'y'=8,'c'=2,'zl'=2,'x'=4] {'y'}, dimensions={0} | all-to-all | bytes 163840 | tf_op jit(solution)/shard_map/all_to_all | solution.py:610
  111.0 11.4 %all_to_all.22 = bf16[8,40,128]{2,1,0:T(8,128)(2,1)S(1)} all-to-all(bf16[8,40,128]{2,1,0:T(8,128)(2,1)S(1)} %broadcast_in_dim.4), channel_id=1, replica_groups=mesh['zh'=4,'y'=8,'c'=2,'zl'=2,'x'=4] {'zh','c'}, dimensions={0} | all-to-all | bytes 163840 | tf_op jit(solution)/shard_map/all_to_all | solution.py:610
  123.0 3.4 %all-to-all-start.3 = ((bf16[8,40,128]{2,1,0:T(8,128)(2,1)}), bf16[8,40,128]{2,1,0:T(8,128)(2,1)S(1)}, u32[]{:S(2)}, u32[]{:S(2)}) async-start(bf16[8,40,128]{2,1,0:T(8,128)(2,1)} %broadcast_in_dim.5), calls=%async_computation.3 | async-start | bytes 163840 | tf_op jit(solution)/shard_map/all_to_all | solution.py:610
  126.4 3.3 %shard_map.160 = bf16[768,128]{1,0:T(8,128)(2,1)} custom-call(s32[12]{0:T(128)S(1)} %copy-done.6, s32[1]{0:T(128)} %bitcast.tile, bf16[2,49,128]{2,1,0:T(8,128)(2,1)S(1)} %copy.20.kernel, bf16[1296,128]{1,0:T(8,128)(2,1)S(1)} %get-tuple-element.73.d1, bf16[1296,128]{1,0:T(8,128)(2,1)S(1)} %get-tuple-element.74.grad0), custom_call_target="tpu_custom_call" | custom-call | flops 9633792 | bytes 1048576 | tf_op jit(solution)/shard_map/pallas_call | solution.py:814
  129.7 4.1 %all-to-all-done.3.full = bf16[8,40,128]{2,1,0:T(8,128)(2,1)S(1)} async-done(((bf16[8,40,128]{2,1,0:T(8,128)(2,1)}), bf16[8,40,128]{2,1,0:T(8,128)(2,1)S(1)}, u32[]{:S(2)}, u32[]{:S(2)}) %all-to-all-start.3) | async-done | bytes 81952 | tf_op jit(solution)/shard_map/all_to_all | solution.py:610
  (31 shorter events, 4.9 us)
Async XLA Ops:
  0.6 31.2 %copy-start = (bf16[2,512,128]{2,1,0:T(8,128)(2,1)S(1)}, bf16[2,512,128]{2,1,0:T(8,128)(2,1)}, u32[]{:S(2)}) copy-start(bf16[2,512,128]{2,1,0:T(8,128)(2,1)} %weight_out.5) | copy-start | bytes 786436
  0.6 31.2 %copy-start.1 = (bf16[2,128,512]{2,1,0:T(8,128)(2,1)S(1)}, bf16[2,128,512]{2,1,0:T(8,128)(2,1)}, u32[]{:S(2)}) copy-start(bf16[2,128,512]{2,1,0:T(8,128)(2,1)} %weight_in.3) | copy-start | bytes 786436
  0.7 1.0 copy-start.2
  1.6 0.9 copy-start.3
  2.6 0.7 copy-start.5
  3.2 28.6 %copy-start.4 = (f32[2,128]{1,0:T(2,128)S(1)}, f32[2,128]{1,0:T(2,128)}, u32[]{:S(2)}) copy-start(f32[2,128]{1,0:T(2,128)} %scale.5) | copy-start | bytes 3076
  3.2 28.6 %copy-start.7 = (f32[2,512]{1,0:T(2,128)S(1)}, f32[2,512]{1,0:T(2,128)}, u32[]{:S(2)}) copy-start(f32[2,512]{1,0:T(2,128)} %bias.1) | copy-start | bytes 12292
  3.2 28.6 %copy-start.8 = (f32[2,128]{1,0:T(2,128)S(1)}, f32[2,128]{1,0:T(2,128)}, u32[]{:S(2)}) copy-start(f32[2,128]{1,0:T(2,128)} %gain.3) | copy-start | bytes 3076
  4.0 14.2 %collective-permute-start = (bf16[192,128]{1,0:T(8,128)(2,1)S(1)}, bf16[192,128]{1,0:T(8,128)(2,1)S(1)}, u32[]{:S(2)}, u32[]{:S(2)}) collective-permute-start(bf16[192,128]{1,0:T(8,128)(2,1)S(1)} %get-tuple-element.45), channel_id=1, source_target_pairs={{0,128},{128,256},{256,384},{384,0},{1,129},{129,257},{257,385},{3... | collective-permute-start | bytes 147464 | tf_op jit(solution)/shard_map/ppermute | solution.py:606
  10.6 8.5 %collective-permute-start.1 = (bf16[192,128]{1,0:T(8,128)(2,1)S(1)}, bf16[192,128]{1,0:T(8,128)(2,1)S(1)}, u32[]{:S(2)}, u32[]{:S(2)}) collective-permute-start(bf16[192,128]{1,0:T(8,128)(2,1)S(1)} %get-tuple-element.46), channel_id=1, source_target_pairs={{0,384},{128,0},{256,128},{384,256},{1,385},{129,1},{257,129},{385... | collective-permute-start | bytes 147464 | tf_op jit(solution)/shard_map/ppermute | solution.py:606
  19.5 7.9 %collective-permute-start.2 = (bf16[696,128]{1,0:T(8,128)(2,1)S(1)}, bf16[696,128]{1,0:T(8,128)(2,1)S(1)}, u32[]{:S(2)}, u32[]{:S(2)}) collective-permute-start(bf16[696,128]{1,0:T(8,128)(2,1)S(1)} %get-tuple-element.49), channel_id=1, source_target_pairs={{0,8},{8,16},{16,24},{24,32},{32,40},{40,48},{48,56},{56,64},{64,7... | collective-permute-start | bytes 534536 | tf_op jit(solution)/shard_map/ppermute | solution.py:606
  24.8 7.1 %collective-permute-start.3 = (bf16[696,128]{1,0:T(8,128)(2,1)S(1)}, bf16[696,128]{1,0:T(8,128)(2,1)S(1)}, u32[]{:S(2)}, u32[]{:S(2)}) collective-permute-start(bf16[696,128]{1,0:T(8,128)(2,1)S(1)} %get-tuple-element.51), channel_id=1, source_target_pairs={{0,504},{8,0},{16,8},{24,16},{32,24},{40,32},{48,40},{56,48},{64,5... | collective-permute-start | bytes 534536 | tf_op jit(solution)/shard_map/ppermute | solution.py:606
  46.2 8.5 %collective-permute-start.4 = (bf16[192,128]{1,0:T(8,128)(2,1)S(1)}, bf16[192,128]{1,0:T(8,128)(2,1)S(1)}, u32[]{:S(2)}, u32[]{:S(2)}) collective-permute-start(bf16[192,128]{1,0:T(8,128)(2,1)S(1)} %get-tuple-element.53), channel_id=1, source_target_pairs={{0,128},{128,256},{256,384},{384,0},{1,129},{129,257},{257,385},{3... | collective-permute-start | bytes 147464 | tf_op jit(solution)/shard_map/ppermute | solution.py:606
  51.6 5.7 %collective-permute-start.5 = (bf16[192,128]{1,0:T(8,128)(2,1)S(1)}, bf16[192,128]{1,0:T(8,128)(2,1)S(1)}, u32[]{:S(2)}, u32[]{:S(2)}) collective-permute-start(bf16[192,128]{1,0:T(8,128)(2,1)S(1)} %get-tuple-element.54), channel_id=1, source_target_pairs={{0,384},{128,0},{256,128},{384,256},{1,385},{129,1},{257,129},{385... | collective-permute-start | bytes 147464 | tf_op jit(solution)/shard_map/ppermute | solution.py:606
  57.6 8.9 %collective-permute-start.6 = (bf16[480,128]{1,0:T(8,128)(2,1)S(1)}, bf16[480,128]{1,0:T(8,128)(2,1)S(1)}, u32[]{:S(2)}, u32[]{:S(2)}) collective-permute-start(bf16[480,128]{1,0:T(8,128)(2,1)S(1)} %get-tuple-element.62), channel_id=1, source_target_pairs={{0,8},{8,16},{16,24},{24,32},{32,40},{40,48},{48,56},{56,64},{64,7... | collective-permute-start | bytes 368648 | tf_op jit(solution)/shard_map/ppermute | solution.py:606
  60.8 6.2 %collective-permute-start.7 = (bf16[480,128]{1,0:T(8,128)(2,1)S(1)}, bf16[480,128]{1,0:T(8,128)(2,1)S(1)}, u32[]{:S(2)}, u32[]{:S(2)}) collective-permute-start(bf16[480,128]{1,0:T(8,128)(2,1)S(1)} %get-tuple-element.64), channel_id=1, source_target_pairs={{0,504},{8,0},{16,8},{24,16},{32,24},{40,32},{48,40},{56,48},{64,5... | collective-permute-start | bytes 368648 | tf_op jit(solution)/shard_map/ppermute | solution.py:606
  77.6 48.8 %copy-start.6 = (s32[12]{0:T(128)S(1)}, s32[12]{0:T(128)}, u32[]{:S(2)}) copy-start(s32[12]{0:T(128)} %flip.7) | copy-start | bytes 148
  123.0 10.8 %all-to-all-start.3 = ((bf16[8,40,128]{2,1,0:T(8,128)(2,1)}), bf16[8,40,128]{2,1,0:T(8,128)(2,1)S(1)}, u32[]{:S(2)}, u32[]{:S(2)}) async-start(bf16[8,40,128]{2,1,0:T(8,128)(2,1)} %broadcast_in_dim.5), calls=%async_computation.3 | async-start | bytes 163840 | tf_op jit(solution)/shard_map/all_to_all | solution.py:610

commit v4 on v3

--- a/solution.py
+++ b/solution.py
@@ -14,8 +14,11 @@
 WIDE = 2 * RIM
 TILE = ("zh", "y", "c")
 DP = ("zl", "x")
-EDGE = 16
+FAR = 2 * WIDE
+EDGE = 24
 LIMIT = 24 << 20
+LEAD_X, LEAD_1, LEAD_0 = FAR + 2, WIDE + 2, RIM
+PAD_X, PAD_H, PAD_1, PAD_0 = 32, 24, 16, 8
 EPSILON = 1e-06
 SQRT_HALF = 0.7071067811865476
 INV_ROOT_TWO_PI = 0.3989422804014327
@@ -65,7 +68,7 @@
     return jnp.broadcast_to(taps[pl.ds(t, 1), :], (8, taps.shape[1]))
 
 
-def convolve(source, width, taps, turned, rows, groups, emit):
+def convolve(source, width, taps, turned, rows, groups, emit, start=0):
     def group(q, carry):
         base = pl.multiple_of(q * 8, 8)
         sums = [None] * rows
@@ -75,7 +78,7 @@
                 tap_row(taps, TAPS - 1 - (KS * i + j) if turned else KS * i + j) for i in range(KS)
             ]
             for r in range(rows + KS - 1):
-                cells = source[pl.ds(base + (r * width + j), 8), :]
+                cells = source[pl.ds(base + (r * width + j + start), 8), :]
                 if j == RIM and 0 <= r - RIM < rows:
                     centers[r - RIM] = cells
                 for i in range(KS):
@@ -122,12 +125,12 @@
         )
 
     def east_of(flag, i):
-        place = jnp.where(i < WIDE, width - WIDE + i, far - RIM + i - WIDE)
-        return jnp.where(i < WIDE + RIM, turned(flag, place), -1)
+        place = jnp.where(i < FAR, width - FAR + i, far - WIDE + i - FAR)
+        return jnp.where(i < FAR + WIDE, turned(flag, place), -1)
 
     def west_of(flag, i):
-        place = jnp.where(i < WIDE, i, width + i - WIDE)
-        return jnp.where(i < WIDE + RIM, turned(flag, place), -1)
+        place = jnp.where(i < FAR, i, width + i - FAR)
+        return jnp.where(i < FAR + WIDE, turned(flag, place), -1)
 
     picks = []
     for flag in (0, 1):
@@ -156,55 +159,52 @@
         up[cells, :] = dot(turn, cotangent[cells, :]).astype(BF16)
 
 
-def widen_row(before, own, after, start, halo, width, total):
+def widener(start, halo, lead, width, total):
     def source_of(i):
-        return jnp.where(
-            i < halo,
-            start + i,
-            jnp.where(
-                i < halo + width,
-                EDGE + i - halo,
-                jnp.where(i < 2 * halo + width, start + EDGE + i - halo, -1),
-            ),
-        )
-
-    both = jnp.concatenate([before, own, after], axis=0)
-    return dot(picker(total, width + 2 * EDGE, source_of), both).astype(BF16)
-
-
-def widen_kernel(height, width, before, after, canon, up, canon_x, up_x, to_next, to_prev):
-    full, slim = width + 16, width + 8
+        c = i - lead
+        inside = jnp.where(c < 0, start + halo + c, jnp.where(c < width, EDGE + c, EDGE + start + c))
+        return jnp.where((c >= -halo) & (c < width + halo), inside, -1)
+
+    return picker(total, width + 2 * EDGE, source_of)
+
+
+def widen_kernel(
+    height, width, before, after, canon, up, canon_x, up_1, up_0, to_next, to_prev
+):
+    pitch_x, pitch_1, pitch_0 = width + PAD_X, width + PAD_1, width + PAD_0
+    pick_x = widener(0, FAR, LEAD_X, width, pitch_x)
+    pick_1 = widener(FAR, WIDE, LEAD_1, width, pitch_1)
+    pick_0 = widener(FAR, WIDE, LEAD_0, width, pitch_0)
+    tail = WIDE * pitch_x
     for r in range(height):
         edge = slice(r * EDGE, (r + 1) * EDGE)
         cells = slice(r * width, (r + 1) * width)
-        a = widen_row(before[edge, :], canon[cells, :], after[edge, :], 0, WIDE, width, full)
-        b = widen_row(before[edge, :], up[cells, :], after[edge, :], WIDE, RIM, width, slim)
-        canon_x[r * full : (r + 1) * full, :] = a
-        up_x[r * slim : (r + 1) * slim, :] = b
+        first, last = before[edge, :], after[edge, :]
+        ups = jnp.concatenate([first, up[cells, :], last], axis=0)
+        a = dot(pick_x, jnp.concatenate([first, canon[cells, :], last], axis=0)).astype(BF16)
+        b = dot(pick_0, ups).astype(BF16)
+        canon_x[r * pitch_x : (r + 1) * pitch_x, :] = a
+        up_1[r * pitch_1 : (r + 1) * pitch_1, :] = dot(pick_1, ups).astype(BF16)
+        up_0[r * pitch_0 : (r + 1) * pitch_0, :] = b
         if r < WIDE:
-            to_prev[r * full : (r + 1) * full, :] = a
+            to_prev[r * pitch_x : (r + 1) * pitch_x, :] = a
         if r < RIM:
-            to_prev[WIDE * full + r * slim : WIDE * full + (r + 1) * slim, :] = b
+            to_prev[tail + r * pitch_0 : tail + (r + 1) * pitch_0, :] = b
         if r >= height - WIDE:
             k = r - (height - WIDE)
-            to_next[k * full : (k + 1) * full, :] = a
+            to_next[k * pitch_x : (k + 1) * pitch_x, :] = a
         if r >= height - RIM:
             k = r - (height - RIM)
-            to_next[WIDE * full + k * slim : WIDE * full + (k + 1) * slim, :] = b
-
-
-def widen_grad_kernel(height, width, before, after, grad, grad_x, to_next, to_prev):
-    full = width + 16
-    for r in range(height):
-        edge = slice(r * EDGE, (r + 1) * EDGE)
-        cells = slice(r * width, (r + 1) * width)
-        a = widen_row(before[edge, :], grad[cells, :], after[edge, :], 0, WIDE, width, full)
-        grad_x[r * full : (r + 1) * full, :] = a
-        if r < WIDE:
-            to_prev[r * full : (r + 1) * full, :] = a
-        if r >= height - WIDE:
-            k = r - (height - WIDE)
-            to_next[k * full : (k + 1) * full, :] = a
+            to_next[tail + k * pitch_0 : tail + (k + 1) * pitch_0, :] = b
+
+
+def own_columns(shape, dim, rows, width):
+    place = lax.broadcasted_iota(jnp.int32, shape, dim)
+    pitch = width + PAD_1
+    column = place
+    for r in range(1, rows):
+        column = column - jnp.where(place >= r * pitch, pitch, 0)
+    return jnp.where((column >= LEAD_1) & (column < LEAD_1 + width), 1.0, 0.0)
 
 
 def join_rows(target, above, middle, below, count, start):
@@ -235,44 +235,53 @@
     hidden0,
     h1,
     grad_conv,
-    east,
-    west,
+    to_next,
+    to_prev,
     scaled1,
     hidden1,
     grad_preact1,
     gain_sum,
     x_scratch,
     taps,
+    conv_flat,
     h1_flat,
     middle,
     conv1,
 ):
-    full, slim = width + 16, width + 8
+    pitch_x, pitch_h, pitch_1 = width + PAD_X, width + PAD_H, width + PAD_1
+    pitch_0 = width + PAD_0
     rim_rows = height + 2 * RIM
-    join_rows(x_scratch, above, canon_x, below, WIDE * full, 0)
+    join_rows(x_scratch, above, canon_x, below, WIDE * pitch_x, 0)
     taps[0:TAPS, :] = kernel[0].astype(F32)
 
     def emit0(base, centers, sums):
         for r in range(rim_rows):
             if centers is not None:
-                h1_flat[pl.ds(base + r * slim, 8), :] = centers[r]
+                h1_flat[pl.ds(base + r * pitch_h, 8), :] = centers[r]
             else:
-                conv0[pl.ds(base + r * slim, 8), :] = sums[r]
-
-    convolve(x_scratch, full, taps, False, rim_rows, slim // 8, emit0)
-
-    chunk0 = 2 * slim
+                conv_flat[pl.ds(base + r * pitch_h, 8), :] = sums[r]
+
+    convolve(x_scratch, pitch_x, taps, False, rim_rows, pitch_h // 8, emit0)
+
+    chunk0 = 2 * pitch_h
+    skip = LEAD_X - RIM - LEAD_0
+
+    def kept(array):
+        rows = [array[r * pitch_h + skip : r * pitch_h + skip + pitch_0] for r in range(2)]
+        return jnp.concatenate(rows, axis=0)
 
     def block0(k, carry):
         cells = pl.ds(pl.multiple_of(k * chunk0, 16), chunk0)
-        normed, _ = moments(conv0[cells, :])
+        saved = pl.ds(pl.multiple_of(k * 2 * pitch_0, 16), 2 * pitch_0)
+        convolved = conv_flat[cells, :]
+        conv0[saved, :] = kept(convolved)
+        normed, _ = moments(convolved)
         scaled = (normed * gain[0:1, :]).astype(BF16)
         preact = dot(scaled, weight_in[0]) + bias[0:1, :]
         value, slope = gelu_parts(preact)
-        hidden = value.astype(BF16)
-        slope0[cells, :] = slope.astype(BF16)
-        hidden0[cells, :] = hidden
-        branch = dot(hidden, weight_out[0])
+        slope0[saved, :] = kept(slope).astype(BF16)
+        hidden0[saved, :] = kept(value).astype(BF16)
+        branch = dot(value.astype(BF16), weight_out[0])
         state = (h1_flat[cells, :] + scale[0:1, :] * branch).astype(BF16)
         h1[cells, :] = state
         h1_flat[cells, :] = state.astype(F32)
@@ -285,17 +294,17 @@
     def emit1(base, centers, sums):
         for r in range(height):
             if centers is not None:
-                middle[pl.ds(base + r * width, 8), :] = centers[r]
+                middle[pl.ds(base + r * pitch_1, 8), :] = centers[r]
             else:
-                conv1[pl.ds(base + r * width, 8), :] = sums[r]
-
-    convolve(h1_flat, slim, taps, False, height, width // 8, emit1)
+                conv1[pl.ds(base + r * pitch_1, 8), :] = sums[r]
+
+    convolve(h1_flat, pitch_h, taps, False, height, pitch_1 // 8, emit1)
 
     gain_sum[...] = jnp.zeros_like(gain_sum)
     chunk_rows = 3
-    chunk1 = chunk_rows * width
-    to_east = picker(EDGE, width, lambda i: jnp.where(i < WIDE, width - WIDE + i, -1))
-    to_west = picker(EDGE, width, lambda i: jnp.where(i < WIDE, i, -1))
+    chunk1 = chunk_rows * pitch_1
+    plain = turner(0, width).astype(F32)
+    flipped = turner(1, width).astype(F32)
 
     def block1(k, carry):
         cells = pl.ds(pl.multiple_of(k * chunk1, 8), chunk1)
@@ -307,7 +316,7 @@
         hidden = value.astype(BF16)
         branch = dot(hidden, weight_out[1])
         scale_row = scale[1:2, :]
-        state = (middle[cells, :] + scale_row * branch).astype(BF16)
+        state = middle[cells, :] + scale_row * branch
         upstream = up[cells, :]
         grad_branch = (upstream.astype(F32) * scale_row).astype(BF16)
         grad_preact = (dot(grad_branch, weight_out[1], ((1,), (1,))) * slope).astype(BF16)
@@ -316,7 +325,9 @@
         grad_preact1[cells, :] = grad_preact
         grad_scaled = dot(grad_preact, weight_in[1], ((1,), (1,)))
         gain_sum[0:1, :] += jnp.sum(
-            grad_scaled * normed, axis=0, keepdims=True
+            grad_scaled * normed * own_columns(normed.shape, 0, chunk_rows, width),
+            axis=0,
+            keepdims=True,
         )
         e = grad_scaled * gain_row
         grad = inv_std * (
@@ -324,25 +335,23 @@
             - jnp.mean(e, axis=-1, keepdims=True)
             - normed * jnp.mean(e * normed, axis=-1, keepdims=True)
         )
-        grad = grad.astype(BF16)
-        grad_conv[cells, :] = grad
+        grad_conv[cells, :] = grad.astype(BF16)
         for r in range(chunk_rows):
             row = k * chunk_rows + r
-            turn = turner(row_flag(flip, tile, row, height, width), width)
-            own = slice(r * width, (r + 1) * width)
-            result[pl.ds(pl.multiple_of(row * width, 8), width), :] = dot(turn, state[own]).astype(
-                BF16
-            )
-            edge = pl.ds(pl.multiple_of(row * EDGE, 8), EDGE)
-            east[edge, :] = dot(to_east, grad[own]).astype(BF16)
-            west[edge, :] = dot(to_west, grad[own]).astype(BF16)
+            flag = row_flag(flip, tile, row, height, width)
+            turn = jnp.where(flag > 0, flipped, plain).astype(BF16)
+            own = state[r * pitch_1 + LEAD_1 : r * pitch_1 + LEAD_1 + width].astype(BF16)
+            result[pl.ds(pl.multiple_of(row * width, 8), width), :] = dot(turn, own).astype(BF16)
         return carry
 
     lax.fori_loop(0, height // chunk_rows, block1, 0)
+    rows = to_prev.shape[0]
+    to_prev[...] = grad_conv[0:rows, :]
+    to_next[...] = grad_conv[height * pitch_1 - rows : height * pitch_1, :]
 
 
 def weights_kernel(
-    scaled, hidden, grad_preact, up, gain_sum, weight_out, scale, big, bias_sum, rows_out, in_sum, out_sum
+    height, width, scaled, hidden, grad_preact, up, gain_sum, weight_out, scale, big, bias_sum, rows_out, in_sum, out_sum
 ):
     in_sum[...] = jnp.zeros_like(in_sum)
     out_sum[...] = jnp.zeros_like(out_sum)
@@ -350,13 +359,18 @@
     rows_out[...] = jnp.zeros_like(rows_out)
     steps = 3
     chunk = scaled.shape[0] // steps
-    ones = jnp.ones((8, chunk), BF16)
+    rows = height // steps
+    ones = own_columns((8, chunk), 1, rows, width).astype(BF16)
+    mask = own_columns((chunk, scaled.shape[1]), 0, rows, width)
+
+    def owned(array):
+        return (array.astype(F32) * mask).astype(BF16)
 
     def step(k, carry):
         cells = pl.ds(pl.multiple_of(k * chunk, 8), chunk)
-        out_sum[...] += dot(up[cells, :], hidden[cells, :], ((0,), (0,)))
+        out_sum[...] += dot(owned(up[cells, :]), hidden[cells, :], ((0,), (0,)))
         bias_sum[...] += dot(ones, grad_preact[cells, :])
-        in_sum[...] += dot(scaled[cells, :], grad_preact[cells, :], ((0,), (0,)))
+        in_sum[...] += dot(owned(scaled[cells, :]), grad_preact[cells, :], ((0,), (0,)))
         return carry
 
     lax.fori_loop(0, steps, step, 0)
@@ -388,10 +402,11 @@
 
 
 def taps_kernel(height, width, h1, grad_conv, out, source, grad):
-    slim = width + 8
     source[...] = h1[...].astype(F32)
     grad[...] = grad_conv[...].astype(F32)
-    tap_sums(source, slim, 0, grad, width, 0, height, width // 8, out)
+    tap_sums(
+        source, width + PAD_H, LEAD_1, grad, width + PAD_1, LEAD_1, height, width // 8, out
+    )
 
 
 def backward_kernel(
@@ -429,10 +444,10 @@
     bias_sum,
     rows_all,
 ):
-    full, slim = width + 16, width + 8
+    full, slim, pitch_1 = width + PAD_X, width + PAD_0, width + PAD_1
     rim_rows = height + 2 * RIM
     channels = gain.shape[1]
-    join_rows(g_scratch, above, grad_x, below, WIDE * full, 0)
+    join_rows(g_scratch, above, grad_x, below, WIDE * pitch_1, 0)
     join_rows(up_flat, x_above, up_x, x_below, RIM * slim, WIDE * full)
     taps[0:TAPS, :] = kernel[1].astype(F32)
 
@@ -442,7 +457,9 @@
                 cells = pl.ds(base + r * slim, 8)
                 d_flat[cells, :] = (up_flat[cells, :] + sums[r]).astype(BF16).astype(F32)
 
-    convolve(g_scratch, full, taps, True, rim_rows, slim // 8, emit1)
+    convolve(
+        g_scratch, pitch_1, taps, True, rim_rows, slim // 8, emit1, LEAD_1 - LEAD_0 - RIM
+    )
 
     in_sum[...] = jnp.zeros_like(in_sum)
     out_sum[...] = jnp.zeros_like(out_sum)
@@ -497,7 +514,7 @@
     tap_sums(
         g_scratch,
         full,
-        RIM * full + RIM,
+        RIM * full + LEAD_X - RIM,
         g0_flat,
         slim,
         RIM * slim + RIM,
@@ -651,7 +668,8 @@
     height, width, channels = fields.shape[1:]
     hidden = weight_in.shape[2]
     members = lax.axis_size(DP)
-    own, full, slim = height * width, width + 16, width + 8
+    own, full, slim = height * width, width + PAD_X, width + PAD_0
+    pitch_h, pitch_1 = width + PAD_H, width + PAD_1
     rim_rows = height + 2 * RIM
     rim = rim_rows * slim
     tall = (height + 2 * WIDE) * full
@@ -661,6 +679,7 @@
     tile = lax.axis_index(TILE).astype(jnp.int32).reshape(1)
 
     cells = shape_of(own, channels)
+    cells_1 = shape_of(height * pitch_1, channels)
     edges = shape_of(height * EDGE, channels)
     given = (face_flip, tile, fields.reshape(own, channels), cotangent.reshape(own, channels))
     east, west = call(functools.partial(edge_kernel, height, width), [edges, edges], 2, 2)(*given)
@@ -669,10 +688,11 @@
     )(*given)
     before = shifted(east, "zh", 1)
     after = shifted(west, "zh", -1)
-    canon_x, up_x, to_next, to_prev = call(
+    canon_x, up_1, up_0, to_next, to_prev = call(
         functools.partial(widen_kernel, height, width),
         [
             shape_of(height * full, channels),
+            shape_of(height * pitch_1, channels),
             shape_of(height * slim, channels),
             shape_of(sent, channels),
             shape_of(sent, channels),
@@ -690,8 +710,8 @@
         hidden0,
         h1,
         grad_conv,
-        east,
-        west,
+        to_next,
+        to_prev,
         scaled1,
         hidden1,
         grad_preact1,
@@ -703,13 +723,13 @@
             shape_of(rim, channels, dtype=F32),
             shape_of(rim, hidden),
             shape_of(rim, hidden),
-            shape_of(rim, channels),
-            cells,
-            edges,
-            edges,
-            cells,
-            shape_of(own, hidden),
-            shape_of(own, hidden),
+            shape_of(rim_rows * pitch_h, channels),
+            cells_1,
+            shape_of(WIDE * pitch_1, channels),
+            shape_of(WIDE * pitch_1, channels),
+            cells_1,
+            shape_of(height * pitch_1, hidden),
+            shape_of(height * pitch_1, hidden),
             shape_of(8, channels, dtype=F32),
         ],
         2,
@@ -717,9 +737,10 @@
         [
             (tall, channels),
             (56, channels),
-            (rim, channels),
-            (own, channels),
-            (own, channels),
+            (rim_rows * pitch_h, channels),
+            (rim_rows * pitch_h, channels),
+            (height * pitch_1, channels),
+            (height * pitch_1, channels),
         ],
     )(
         face_flip,
@@ -727,7 +748,7 @@
         above,
         canon_x,
         below,
-        up,
+        up_1,
         kernel,
         ln_gain,
         weight_in,
@@ -735,10 +756,8 @@
         weight_out,
         layer_scale,
     )
-    before = shifted(east, "zh", 1)
-    after = shifted(west, "zh", -1)
     big1, bias1, rows1 = call(
-        weights_kernel,
+        functools.partial(weights_kernel, height, width),
         [
             shape_of(members, strips, big_rows, channels),
             shape_of(8, hidden, dtype=F32),
@@ -748,26 +767,15 @@
         7,
         [sums, sums],
         work(4 * own * hidden * channels),
-    )(scaled1, hidden1, grad_preact1, up, gain1, weight_out, layer_scale)
-    due, big1 = lax.optimization_barrier((grad_conv, big1))
+    )(scaled1, hidden1, grad_preact1, up_1, gain1, weight_out, layer_scale)
     (taps1,) = call(
         functools.partial(taps_kernel, height, width),
         [shape_of(56, channels, dtype=F32)],
         0,
         2,
-        [(rim, channels), (own, channels)],
+        [(rim_rows * pitch_h, channels), (height * pitch_1, channels)],
         work(2 * TAPS * own * channels),
     )(h1, grad_conv)
-    grad_x, to_next, to_prev = call(
-        functools.partial(widen_grad_kernel, height, width),
-        [
-            shape_of(height * full, channels),
-            shape_of(WIDE * full, channels),
-            shape_of(WIDE * full, channels),
-        ],
-        0,
-        3,
-    )(before, after, due)
     grad_above = shifted(to_next, TILE, 1)
     grad_below = shifted(to_prev, TILE, -1)
     d1, grad0, packed = call(
@@ -792,12 +800,12 @@
         ],
     )(
         grad_above,
-        grad_x,
+        grad_conv,
         grad_below,
         above,
         canon_x,
         below,
-        up_x,
+        up_0,
         kernel,
         ln_gain,
         weight_in,

time: 135 us -> 128 us (0.948)
  starting transfers between devices: 38.5 us -> 31.4 us
  waiting for transfers between devices: 12.5 us -> 10.6 us
  blocking collectives: 44.6 us -> 46 us
    ppermute x8 -> x6, starting transfers between devices: 35.1 us -> 28 us  [shifted(): lax.ppermute(block, axis, [(i, (i + distance) % count) for i in range(cou...]
    ppermute x8 -> x6, waiting for transfers between devices: 8.39 us -> 6.56 us  [shifted(): lax.ppermute(block, axis, [(i, (i + distance) % count) for i in range(cou...]
    all_to_all x3, blocking collectives: 44.6 us -> 46 us  [exchanged(): return lax.all_to_all(blocks, axis, 0, 0, tiled=True)]
    unnamed x19 -> x21, local copies, waits for them, and re-layouts: 3.33 us -> 2.59 us
  transfers between devices with their start and end apart: 9 -> 7, of which waited for: 5 -> 4; matrix products, arithmetic and copies ran while one was open for 1% -> 0% of each run, Pallas kernels for 5% -> 6%
where the time goes in v4:
time: 128 us; the launch traced here: 127 us
  blocking collectives  46 us (36%)
  Pallas kernels  35.2 us (28%)
  starting transfers between devices  31.4 us (25%)
  waiting for transfers between devices  10.6 us (8%)
  local copies, waits for them, and re-layouts  3.25 us (3%)
    all_to_all x3, blocking collectives, exchanged(): return lax.all_to_all(blocks, axis, 0, 0, tiled=True)  46 us
    ppermute x6, starting transfers between devices, shifted(): lax.ppermute(block, axis, [(i, (i + distance) % count) for i in range(cou...  28 us
    pallas_call x1, Pallas kernels, on_device(): call(functools.partial(forward_kernel, height, width), [cells, shape_of(r...  15.2 us
    pallas_call x1, Pallas kernels, on_device(): call(functools.partial(backward_kernel, height, width), [shape_of(rim, ch...  10.6 us
    ppermute x6, waiting for transfers between devices, shifted(): lax.ppermute(block, axis, [(i, (i + distance) % count) for i in range(cou...  6.56 us
    all_to_all x1, waiting for transfers between devices, exchanged(): return lax.all_to_all(blocks, axis, 0, 0, tiled=True)  4.08 us
    all_to_all x1, starting transfers between devices, exchanged(): return lax.all_to_all(blocks, axis, 0, 0, tiled=True)  3.36 us
    pallas_call x1, Pallas kernels, on_device(): call(functools.partial(spread_kernel, height, width), [cells], 2, 3, [(56...  3.32 us
  transfers between devices with their start and end apart: 7, of which 4 were waited for; matrix products, arithmetic and copies ran while one was open for 0% of the time, Pallas kernels for 6%

profile of v4, /device:TPU:1, one launch (start us, length us, event | category | flops | bytes accessed | tf_op | source)
XLA Modules:
  0.0 127.4 jit_solution(3534567065657513538)
XLA Ops:
  0.7 1.0 copy-done.2
  1.6 0.9 copy-done.3
  3.2 0.8 shard_map.152
  4.0 6.6 %collective-permute-start = (bf16[288,128]{1,0:T(8,128)(2,1)S(1)}, bf16[288,128]{1,0:T(8,128)(2,1)S(1)}, u32[]{:S(2)}, u32[]{:S(2)}) collective-permute-start(bf16[288,128]{1,0:T(8,128)(2,1)S(1)} %get-tuple-element.41), channel_id=1, source_target_pairs={{0,128},{128,256},{256,384},{384,0},{1,129},{129,257},{257,385},{3... | collective-permute-start | bytes 221192 | tf_op jit(solution)/shard_map/ppermute | solution.py:623
  10.7 6.8 %collective-permute-start.1 = (bf16[288,128]{1,0:T(8,128)(2,1)S(1)}, bf16[288,128]{1,0:T(8,128)(2,1)S(1)}, u32[]{:S(2)}, u32[]{:S(2)}) collective-permute-start(bf16[288,128]{1,0:T(8,128)(2,1)S(1)} %get-tuple-element.42), channel_id=1, source_target_pairs={{0,384},{128,0},{256,128},{384,256},{1,385},{129,1},{257,129},{385... | collective-permute-start | bytes 221192 | tf_op jit(solution)/shard_map/ppermute | solution.py:623
  17.4 0.8 shard_map.153
  18.3 1.2 collective-permute-done.1.after
  19.9 6.3 %collective-permute-start.2 = (bf16[792,128]{1,0:T(8,128)(2,1)S(1)}, bf16[792,128]{1,0:T(8,128)(2,1)S(1)}, u32[]{:S(2)}, u32[]{:S(2)}) collective-permute-start(bf16[792,128]{1,0:T(8,128)(2,1)S(1)} %get-tuple-element.45), channel_id=1, source_target_pairs={{0,8},{8,16},{16,24},{24,32},{32,40},{40,48},{48,56},{56,64},{64,7... | collective-permute-start | bytes 608264 | tf_op jit(solution)/shard_map/ppermute | solution.py:623
  26.2 1.9 %collective-permute-start.3 = (bf16[792,128]{1,0:T(8,128)(2,1)S(1)}, bf16[792,128]{1,0:T(8,128)(2,1)S(1)}, u32[]{:S(2)}, u32[]{:S(2)}) collective-permute-start(bf16[792,128]{1,0:T(8,128)(2,1)S(1)} %get-tuple-element.47), channel_id=1, source_target_pairs={{0,504},{8,0},{16,8},{24,16},{32,24},{40,32},{48,40},{56,48},{64,5... | collective-permute-start | bytes 608264 | tf_op jit(solution)/shard_map/ppermute | solution.py:623
  28.2 0.7 collective-permute-done.2.above.x_above
  28.9 4.7 %collective-permute-done.3.below.x_below = bf16[792,128]{1,0:T(8,128)(2,1)S(1)} collective-permute-done((bf16[792,128]{1,0:T(8,128)(2,1)S(1)}, bf16[792,128]{1,0:T(8,128)(2,1)S(1)}, u32[]{:S(2)}, u32[]{:S(2)}) %collective-permute-start.3) | collective-permute-done | bytes 202784 | tf_op jit(solution)/shard_map/ppermute | solution.py:623
  33.6 15.2 %shard_map.155 = (bf16[768,128]{1,0:T(8,128)(2,1)}, f32[1296,128]{1,0:T(8,128)S(1)}, bf16[1296,512]{1,0:T(8,128)(2,1)S(1)}, bf16[1296,512]{1,0:T(8,128)(2,1)S(1)...) custom-call(s32[12]{0:T(128)S(1)} %copy-done.5, ...), custom_call_target="tpu_custom_call" | custom-call | tf_op jit(solution)/shard_map/pallas_call | solution.py:719
  48.8 1.9 %collective-permute-start.4 = (bf16[480,128]{1,0:T(8,128)(2,1)S(1)}, bf16[480,128]{1,0:T(8,128)(2,1)S(1)}, u32[]{:S(2)}, u32[]{:S(2)}) collective-permute-start(bf16[480,128]{1,0:T(8,128)(2,1)S(1)} %get-tuple-element.50), channel_id=1, source_target_pairs={{0,8},{8,16},{16,24},{24,32},{32,40},{40,48},{48,56},{56,64},{64,7... | collective-permute-start | bytes 368648 | tf_op jit(solution)/shard_map/ppermute | solution.py:623
  50.7 4.5 %collective-permute-start.5 = (bf16[480,128]{1,0:T(8,128)(2,1)S(1)}, bf16[480,128]{1,0:T(8,128)(2,1)S(1)}, u32[]{:S(2)}, u32[]{:S(2)}) collective-permute-start(bf16[480,128]{1,0:T(8,128)(2,1)S(1)} %get-tuple-element.52), channel_id=1, source_target_pairs={{0,504},{8,0},{16,8},{24,16},{32,24},{40,32},{48,40},{56,48},{64,5... | collective-permute-start | bytes 368648 | tf_op jit(solution)/shard_map/ppermute | solution.py:623
  55.2 1.8 %shard_map.157.taps1 = f32[56,128]{1,0:T(8,128)S(1)} custom-call(bf16[1584,128]{1,0:T(8,128)(2,1)S(1)} %get-tuple-element.64.h1, bf16[960,128]{1,0:T(8,128)(2,1)S(1)} %get-tuple-element.51.grad_conv.grad_x), custom_call_target="tpu_custom_call" | custom-call | flops 9633792 | bytes 1048576 | tf_op jit(solution)/shard_map/pallas_call | solution.py:771
  57.0 1.4 %shard_map.156 = (bf16[8,4,32,128]{3,2,1,0:T(8,128)(2,1)S(1)}, f32[8,512]{1,0:T(8,128)S(1)}, f32[64,128]{1,0:T(8,128)S(1)}) custom-call(bf16[960,128]{1,0:T(8,128)(2,1)S(1)} %get-tuple-element.57.scaled, bf16[960,512]{1,0:T(8,128)(2,1)S(1)} %get-tuple-element.58.hidden, bf16[960,512]{1,0:T(8,128)(2,1)S(1)} %get-tuple-element.59.grad_preact, ...), custom_call_target="tpu_custom_call" | custom-call | flops 201326592 | bytes 1048576 | tf_op jit(solution)/shard_map/pallas_call | solution.py:759
  58.5 10.6 %shard_map.158 = (bf16[1296,128]{1,0:T(8,128)(2,1)S(1)}, bf16[1296,128]{1,0:T(8,128)(2,1)S(1)}, bf16[8,8,40,128]{3,2,1,0:T(8,128)(2,1)S(1)}) custom-call(bf16[480,128]{1,0:T(8,128)(2,1)S(1)} %collective-permute-done.4.above, bf16[960,128]{1,0:T(8,128)(2,1)S(1)} %get-tuple-element.51.grad_conv.grad_x, bf16[480,128]{1,0:T(8,128)(2,1)S(1)} %collective-permute-done.5.below, ...), custom_call_target="tpu_custom_call" | custom-call | tf_op jit(solution)/shard_map/pallas_call | solution.py:781
  69.1 12.1 %all_to_all.20 = bf16[8,8,40,128]{3,2,1,0:T(8,128)(2,1)S(1)} all-to-all(bf16[8,8,40,128]{3,2,1,0:T(8,128)(2,1)S(1)} %get-tuple-element.67), channel_id=1, replica_groups=mesh['zh'=4,'y'=8,'c'=2,'zl'=2,'x'=4] {'zl','x'}, dimensions={0} | all-to-all | bytes 1310720 | tf_op jit(solution)/shard_map/all_to_all | solution.py:627
  81.3 20.8 %all_to_all.21 = bf16[8,40,128]{2,1,0:T(8,128)(2,1)S(1)} all-to-all(bf16[8,40,128]{2,1,0:T(8,128)(2,1)S(1)} %reduce_sum.36), channel_id=1, replica_groups=mesh['zh'=4,'y'=8,'c'=2,'zl'=2,'x'=4] {'y'}, dimensions={0} | all-to-all | bytes 163840 | tf_op jit(solution)/shard_map/all_to_all | solution.py:627
  102.1 13.2 %all_to_all.22 = bf16[8,40,128]{2,1,0:T(8,128)(2,1)S(1)} all-to-all(bf16[8,40,128]{2,1,0:T(8,128)(2,1)S(1)} %broadcast_in_dim.4), channel_id=1, replica_groups=mesh['zh'=4,'y'=8,'c'=2,'zl'=2,'x'=4] {'zh','c'}, dimensions={0} | all-to-all | bytes 163840 | tf_op jit(solution)/shard_map/all_to_all | solution.py:627
  115.9 3.4 %all-to-all-start.3 = ((bf16[8,40,128]{2,1,0:T(8,128)(2,1)}), bf16[8,40,128]{2,1,0:T(8,128)(2,1)S(1)}, u32[]{:S(2)}, u32[]{:S(2)}) async-start(bf16[8,40,128]{2,1,0:T(8,128)(2,1)} %broadcast_in_dim.5), calls=%async_computation.3 | async-start | bytes 163840 | tf_op jit(solution)/shard_map/all_to_all | solution.py:627
  119.3 3.3 %shard_map.159 = bf16[768,128]{1,0:T(8,128)(2,1)} custom-call(s32[12]{0:T(128)S(1)} %copy-done.6, s32[1]{0:T(128)} %bitcast.tile, bf16[2,49,128]{2,1,0:T(8,128)(2,1)S(1)} %copy.20.kernel, bf16[1296,128]{1,0:T(8,128)(2,1)S(1)} %get-tuple-element.65.d1, bf16[1296,128]{1,0:T(8,128)(2,1)S(1)} %get-tuple-element.66.grad0), custom_call_target="tpu_custom_call" | custom-call | flops 9633792 | bytes 1048576 | tf_op jit(solution)/shard_map/pallas_call | solution.py:822
  122.6 4.1 %all-to-all-done.3.full = bf16[8,40,128]{2,1,0:T(8,128)(2,1)S(1)} async-done(((bf16[8,40,128]{2,1,0:T(8,128)(2,1)}), bf16[8,40,128]{2,1,0:T(8,128)(2,1)S(1)}, u32[]{:S(2)}, u32[]{:S(2)}) %all-to-all-start.3) | async-done | bytes 81952 | tf_op jit(solution)/shard_map/all_to_all | solution.py:627
  126.7 0.7 shard_map.160
  (28 shorter events, 2.0 us)
Async XLA Ops:
  0.6 32.9 %copy-start = (bf16[2,512,128]{2,1,0:T(8,128)(2,1)S(1)}, bf16[2,512,128]{2,1,0:T(8,128)(2,1)}, u32[]{:S(2)}) copy-start(bf16[2,512,128]{2,1,0:T(8,128)(2,1)} %weight_out.5) | copy-start | bytes 786436
  0.6 32.9 %copy-start.1 = (bf16[2,128,512]{2,1,0:T(8,128)(2,1)S(1)}, bf16[2,128,512]{2,1,0:T(8,128)(2,1)}, u32[]{:S(2)}) copy-start(bf16[2,128,512]{2,1,0:T(8,128)(2,1)} %weight_in.3) | copy-start | bytes 786436
  0.7 1.0 copy-start.2
  1.6 0.9 copy-start.3
  2.6 0.7 copy-start.5
  3.2 24.9 %copy-start.9 = (bf16[2,49,128]{2,0,1:T(2,128)(2,1)S(1)}, bf16[2,49,128]{2,0,1:T(2,128)(2,1)}, u32[]{:S(2)}) copy-start(bf16[2,49,128]{2,0,1:T(2,128)(2,1)} %param.12) | copy-start | bytes 75268
  3.2 30.3 %copy-start.4 = (f32[2,128]{1,0:T(2,128)S(1)}, f32[2,128]{1,0:T(2,128)}, u32[]{:S(2)}) copy-start(f32[2,128]{1,0:T(2,128)} %scale.5) | copy-start | bytes 3076
  3.2 30.4 %copy-start.7 = (f32[2,512]{1,0:T(2,128)S(1)}, f32[2,512]{1,0:T(2,128)}, u32[]{:S(2)}) copy-start(f32[2,512]{1,0:T(2,128)} %bias.1) | copy-start | bytes 12292
  3.2 30.4 %copy-start.8 = (f32[2,128]{1,0:T(2,128)S(1)}, f32[2,128]{1,0:T(2,128)}, u32[]{:S(2)}) copy-start(f32[2,128]{1,0:T(2,128)} %gain.3) | copy-start | bytes 3076
  4.0 14.2 %collective-permute-start = (bf16[288,128]{1,0:T(8,128)(2,1)S(1)}, bf16[288,128]{1,0:T(8,128)(2,1)S(1)}, u32[]{:S(2)}, u32[]{:S(2)}) collective-permute-start(bf16[288,128]{1,0:T(8,128)(2,1)S(1)} %get-tuple-element.41), channel_id=1, source_target_pairs={{0,128},{128,256},{256,384},{384,0},{1,129},{129,257},{257,385},{3... | collective-permute-start | bytes 221192 | tf_op jit(solution)/shard_map/ppermute | solution.py:623
  10.7 8.8 %collective-permute-start.1 = (bf16[288,128]{1,0:T(8,128)(2,1)S(1)}, bf16[288,128]{1,0:T(8,128)(2,1)S(1)}, u32[]{:S(2)}, u32[]{:S(2)}) collective-permute-start(bf16[288,128]{1,0:T(8,128)(2,1)S(1)} %get-tuple-element.42), channel_id=1, source_target_pairs={{0,384},{128,0},{256,128},{384,256},{1,385},{129,1},{257,129},{385... | collective-permute-start | bytes 221192 | tf_op jit(solution)/shard_map/ppermute | solution.py:623
  19.9 9.0 %collective-permute-start.2 = (bf16[792,128]{1,0:T(8,128)(2,1)S(1)}, bf16[792,128]{1,0:T(8,128)(2,1)S(1)}, u32[]{:S(2)}, u32[]{:S(2)}) collective-permute-start(bf16[792,128]{1,0:T(8,128)(2,1)S(1)} %get-tuple-element.45), channel_id=1, source_target_pairs={{0,8},{8,16},{16,24},{24,32},{32,40},{40,48},{48,56},{56,64},{64,7... | collective-permute-start | bytes 608264 | tf_op jit(solution)/shard_map/ppermute | solution.py:623
  26.2 7.3 %collective-permute-start.3 = (bf16[792,128]{1,0:T(8,128)(2,1)S(1)}, bf16[792,128]{1,0:T(8,128)(2,1)S(1)}, u32[]{:S(2)}, u32[]{:S(2)}) collective-permute-start(bf16[792,128]{1,0:T(8,128)(2,1)S(1)} %get-tuple-element.47), channel_id=1, source_target_pairs={{0,504},{8,0},{16,8},{24,16},{32,24},{40,32},{48,40},{56,48},{64,5... | collective-permute-start | bytes 608264 | tf_op jit(solution)/shard_map/ppermute | solution.py:623
  48.8 9.7 %collective-permute-start.4 = (bf16[480,128]{1,0:T(8,128)(2,1)S(1)}, bf16[480,128]{1,0:T(8,128)(2,1)S(1)}, u32[]{:S(2)}, u32[]{:S(2)}) collective-permute-start(bf16[480,128]{1,0:T(8,128)(2,1)S(1)} %get-tuple-element.50), channel_id=1, source_target_pairs={{0,8},{8,16},{16,24},{24,32},{32,40},{40,48},{48,56},{56,64},{64,7... | collective-permute-start | bytes 368648 | tf_op jit(solution)/shard_map/ppermute | solution.py:623
  50.7 7.7 %collective-permute-start.5 = (bf16[480,128]{1,0:T(8,128)(2,1)S(1)}, bf16[480,128]{1,0:T(8,128)(2,1)S(1)}, u32[]{:S(2)}, u32[]{:S(2)}) collective-permute-start(bf16[480,128]{1,0:T(8,128)(2,1)S(1)} %get-tuple-element.52), channel_id=1, source_target_pairs={{0,504},{8,0},{16,8},{24,16},{32,24},{40,32},{48,40},{56,48},{64,5... | collective-permute-start | bytes 368648 | tf_op jit(solution)/shard_map/ppermute | solution.py:623
  69.1 50.2 %copy-start.6 = (s32[12]{0:T(128)S(1)}, s32[12]{0:T(128)}, u32[]{:S(2)}) copy-start(s32[12]{0:T(128)} %flip.7) | copy-start | bytes 148
  115.9 10.8 %all-to-all-start.3 = ((bf16[8,40,128]{2,1,0:T(8,128)(2,1)}), bf16[8,40,128]{2,1,0:T(8,128)(2,1)S(1)}, u32[]{:S(2)}, u32[]{:S(2)}) async-start(bf16[8,40,128]{2,1,0:T(8,128)(2,1)} %broadcast_in_dim.5), calls=%async_computation.3 | async-start | bytes 163840 | tf_op jit(solution)/shard_map/all_to_all | solution.py:627
